TPU v7x, 128 devices: a whole 4x4x4 slice. The times are simulated.
128 devices in a mesh: oct: 2 (over core), sub: 64 (over x, z, y).
Axes of the slice: x: 4, y: 4, z: 4, core: 2. Of those that a mesh axis runs over, the one named last changes fastest.
Arguments:
- coefficients: float32 [2048, 4096], P(('oct', 'sub')), may hold values from -6 to 6
- potential: float32 [2048, 4096], P(('oct', 'sub')), may hold values from 0.2 to 2
- to_values: float32 [16, 16], replicated, may hold values from -1.5 to 1.5
- x_kernels: bfloat16 [20, 48, 16], replicated, may hold values from -0.5 to 0.5
- yz_kernels: bfloat16 [256, 46080], replicated, may hold values from -0.046875 to 0.046875
- two_scale: float32 [2, 16, 16], replicated, may hold values from -1 to 1
- disp_ids: int32 [2048, 16], P(('oct', 'sub')), may hold values from -1 to 26, as said below
- dest_box: int32 [2048, 16], P(('oct', 'sub')), may hold values from -1 to 2047, as said below
- parent_of: int32 [2048], P(('oct', 'sub')), may hold values from 0 to 255, as said below
- child_octant: int32 [2048], P(('oct', 'sub')), may hold values from 0 to 7
Outputs:
- next_field: float32 [2048, 4096], P(('oct', 'sub'))
- parents: float32 [256, 4096], P(('oct', 'sub'))
Inputs may be any that keep to these rules, and one draw needn't show every extreme that they name: `disp_ids`: -1 marks an empty slot, exactly where dest_box is -1; in every row the live slots come first, 4 or more of them. `dest_box`: among the live slots of one aligned block of 16 rows, at most 2 name boxes of any one aligned block of 16 boxes; some box block receives exactly 2 from every row block. Every parent is named by exactly 8 boxes, whose child_octant values are 0 to 7; parent_of[b] // 128 == b // 1024. Within one aligned block of 16 boxes, at most 1 box has its parent in any one aligned block of 2 parents, and some parent block is named by exactly 1 of them.
All inputs are finite; a program needn't handle non-finite values.
Results may differ from a plain program's by a relative error of at most 0.018.
Values may be sent and summed in bfloat16 or wider, within the bound.
A program may use at most 192 MiB of HBM per device.

v0:
```python
import jax
import jax.numpy as jnp
from jax import lax
from jax.sharding import PartitionSpec as P

ITERS = 2


def apply_pair(blocks, along_x, pair, order_k):
    highest = lax.Precision.HIGHEST
    rows_total = blocks.shape[0]
    plane_size = order_k * order_k
    inner = jnp.dot(blocks.reshape(rows_total * order_k, plane_size), pair, precision=highest)
    inner = inner.reshape(rows_total, order_k, plane_size)
    return jnp.einsum("ix,bxr->bir", along_x, inner, precision=highest).reshape(
        rows_total, plane_size * order_k
    )


def quad_of(filters):
    order_k = filters.shape[1]
    return jnp.einsum("cjy,dkz->yzcdjk", filters, filters, precision=lax.Precision.HIGHEST).reshape(
        order_k * order_k, 4 * order_k * order_k
    )


def lift_boxes(blocks, filters, quad, octant):
    highest = lax.Precision.HIGHEST
    rows_total = blocks.shape[0]
    order_k = filters.shape[1]
    plane_size = order_k * order_k
    inner = jnp.dot(blocks.reshape(rows_total * order_k, plane_size), quad, precision=highest)
    inner = inner.reshape(rows_total, order_k, 4, plane_size)
    select = (octant[:, None] % 4 == jnp.arange(4)[None, :]).astype(jnp.float32)
    inner = jnp.einsum("bxcr,bc->bxr", inner, select, precision=highest)
    along_x = jnp.where((octant // 4 == 1)[:, None, None], filters[1][None], filters[0][None])
    return jnp.einsum("bix,bxr->bir", along_x, inner, precision=highest).reshape(
        rows_total, plane_size * order_k
    )


def shards(
    coefficients,
    potential,
    to_values,
    x_kernels,
    yz_kernels,
    two_scale,
    disp_ids,
    dest_box,
    parent_of,
    child_octant,
):
    highest = lax.Precision.HIGHEST
    box_count = coefficients.shape[0]
    order_k = to_values.shape[0]
    plane_size = order_k * order_k
    cube_size = plane_size * order_k
    slot_count = disp_ids.shape[1]
    term_count = x_kernels.shape[0]
    oct_count = lax.axis_size("oct")
    sub_count = lax.axis_size("sub")
    devices_all = oct_count * sub_count
    capacity = box_count * slot_count // devices_all
    block_boxes = 16
    count_blocks = box_count // block_boxes
    parent_local = box_count // 8
    per_group = sub_count * parent_local
    value_pair = jnp.einsum("jy,kz->yzjk", to_values, to_values, precision=highest).reshape(
        plane_size, plane_size
    )
    back_pair = jnp.einsum("yj,zk->yzjk", to_values, to_values, precision=highest).reshape(
        plane_size, plane_size
    )
    flipped = jnp.swapaxes(two_scale, 1, 2)
    lift_quad = quad_of(two_scale)
    drop_quad = quad_of(flipped)
    flat_dest = dest_box.reshape(-1)
    owner_ids = flat_dest // box_count
    is_live = flat_dest >= 0
    hits = (owner_ids[:, None] == jnp.arange(devices_all, dtype=jnp.int32)[None, :]).astype(
        jnp.int32
    )
    before = jnp.cumsum(hits, axis=0) - hits
    rank_ids = jnp.sum(before * hits, axis=1)
    slot_index = jnp.where(is_live, owner_ids * capacity + rank_ids, devices_all * capacity)
    local_box = flat_dest - owner_ids * box_count
    label_row = (
        jnp.zeros((devices_all * capacity + 1,), jnp.bfloat16)
        .at[slot_index]
        .set(local_box.astype(jnp.bfloat16))[:-1]
    )
    local_parents = parent_of - lax.axis_index("oct") * per_group
    member_up = (jnp.arange(per_group, dtype=jnp.int32)[:, None] == local_parents[None, :]).astype(
        jnp.float32
    )
    box_ids = jnp.arange(box_count, dtype=jnp.int32)

    def convolve(carry_none, block_items):
        source_blk, disp_blk = block_items
        partial_value = jnp.dot(
            source_blk.reshape(block_boxes * order_k, plane_size),
            yz_kernels,
            preferred_element_type=jnp.float32,
        ).astype(jnp.bfloat16)
        partial_value = partial_value.reshape(block_boxes, order_k, term_count, 9 * plane_size)
        convolved = jnp.einsum(
            "bxmr,max->bar", partial_value, x_kernels, preferred_element_type=jnp.float32
        )
        convolved = (
            convolved.reshape(block_boxes, 3, order_k, 9, plane_size)
            .transpose(0, 1, 3, 2, 4)
            .reshape(block_boxes, 27, cube_size)
        )
        picked = jnp.take_along_axis(
            convolved, jnp.maximum(disp_blk, 0)[:, :, None], axis=1
        ).astype(jnp.bfloat16)
        return (carry_none, picked)

    current = coefficients
    own_parents = jnp.zeros((parent_local, cube_size), jnp.float32)
    for iteration in range(ITERS):
        values = apply_pair(current, to_values, value_pair, order_k)
        product = values * (potential + 0.25 * values * values)
        source = apply_pair(product, to_values.T, back_pair, order_k).astype(jnp.bfloat16)
        unused, picked = lax.scan(
            convolve,
            jnp.zeros((), jnp.int32),
            (
                source.reshape(count_blocks, block_boxes, cube_size),
                disp_ids.reshape(count_blocks, block_boxes, slot_count),
            ),
        )
        outgoing = picked.reshape(box_count * slot_count, cube_size)
        send_tiles = (
            jnp.zeros((devices_all * capacity + 1, cube_size), jnp.bfloat16)
            .at[slot_index]
            .set(outgoing)[:-1]
        )
        arrived, arrived_labels = (
            lax.all_to_all(
                send_tiles.reshape(devices_all, capacity, cube_size),
                ("oct", "sub"),
                split_axis=0,
                concat_axis=0,
                tiled=True,
            ),
            lax.all_to_all(
                label_row.reshape(devices_all, capacity),
                ("oct", "sub"),
                split_axis=0,
                concat_axis=0,
                tiled=True,
            ),
        )
        incoming = arrived.reshape(devices_all * capacity, cube_size)
        arrived_boxes = arrived_labels.reshape(-1).astype(jnp.int32)
        member_in = (arrived_boxes[None, :] == box_ids[:, None]).astype(jnp.bfloat16)
        gathered = jnp.dot(member_in, incoming, preferred_element_type=jnp.float32)
        lifted = lift_boxes(gathered, two_scale, lift_quad, child_octant)
        contrib = jnp.dot(member_up, lifted, precision=highest)
        own_parents = lax.psum_scatter(contrib, "sub", scatter_dimension=0, tiled=True)
        everyone = lax.all_gather(
            own_parents.astype(jnp.bfloat16), "sub", axis=0, tiled=True
        ).astype(own_parents.dtype)
        matched = jnp.take(everyone, local_parents, axis=0)
        current = gathered - lift_boxes(matched, flipped, drop_quad, child_octant)
    return (current, own_parents)


def solution(mesh):
    placed = (
        P(("oct", "sub"), None),
        P(("oct", "sub"), None),
        P(),
        P(),
        P(),
        P(),
        P(("oct", "sub"), None),
        P(("oct", "sub"), None),
        P(("oct", "sub")),
        P(("oct", "sub")),
    )
    return jax.shard_map(
        shards,
        mesh=mesh,
        in_specs=placed,
        out_specs=(P(("oct", "sub"), None), P(("oct", "sub"), None)),
        check_vma=False,
    )
```

profile of v0, /device:TPU:0, one launch (start us, length us, event | category | flops | bytes accessed | tf_op | source)
XLA Modules:
  0.0 983.5 jit_solution(8387002277231726505)
XLA Ops:
  13.1 11.9 %all-to-all-start = ((bf16[128,1,2]{2,1,0:T(2,128)(2,1)}), bf16[128,1,2]{2,1,0:T(2,128)(2,1)}, u32[]{:S(2)}, u32[]{:S(2)}) async-start(bf16[128,1,2]{2,1,0:T(2,128)(2,1)} %all_to_all.17), calls=%async_computation | async-start | bytes 131072 | tf_op jit(solution)/shard_map/all_to_all | solution.py:148
  35.0 20.6 %convolution_convert_fusion.1 = bf16[256,46080]{1,0:T(8,128)(2,1)} fusion(bf16[256,256]{1,0:T(8,128)(2,1)S(1)} %bitcast.221, bf16[256,46080]{1,0:T(8,128)(2,1)} %param.18), kind=kOutput, calls=%fused_computation.8 | convolution fusion | flops 6051594240 | bytes 47316992 | tf_op jit(solution)/shard_map/while/body/eval_jaxpr/dot_general | solution.py:101
  55.6 32.9 %reshape.316 = bf16[16,16,20,2304]{3,2,1,0:T(8,128)(2,1)} reshape(bf16[256,46080]{1,0:T(8,128)(2,1)} %convolution_convert_fusion.1) | data formatting | bytes 47185920 | tf_op jit(solution)/shard_map/while/body/eval_jaxpr/reshape | solution.py:106
  88.5 11.5 %convolution_bitcast_fusion.1 = bf16[16,48,2304]{2,1,0:T(8,128)(2,1)S(1)} fusion(bf16[16,16,20,2304]{3,2,1,0:T(8,128)(2,1)} %reshape.316, bf16[20,48,16]{1,2,0:T(8,128)(2,1)} %param.17), kind=kOutput, calls=%fused_computation.12 | convolution fusion | flops 1132462080 | bytes 27162624 | tf_op jit(solution)/shard_map/while/body/eval_jaxpr/bxmr,max->bar/dot_general | solution.py:107
  104.9 6.0 copy.44
  110.9 5.4 reshape.318
  117.1 8.5 gather_fusion
  140.2 9.9 %all-to-all-start.1 = ((bf16[128,2,4096]{2,1,0:T(2,128)(2,1)}), bf16[128,2,4096]{2,1,0:T(2,128)(2,1)S(1)}, u32[]{:S(2)}, u32[]{:S(2)}) async-start(bf16[128,2,4096]{2,1,0:T(2,128)(2,1)} %reshape.320), calls=%async_computation.1 | async-start | bytes 4194304 | tf_op jit(solution)/shard_map/all_to_all | solution.py:141
  154.6 8.7 reshape.322
  167.7 12.3 %all-to-all-done.1 = bf16[128,2,4096]{2,1,0:T(2,128)(2,1)S(1)} async-done(((bf16[128,2,4096]{2,1,0:T(2,128)(2,1)}), bf16[128,2,4096]{2,1,0:T(2,128)(2,1)S(1)}, u32[]{:S(2)}, u32[]{:S(2)}) %all-to-all-start.1) | async-done | bytes 2097184 | tf_op jit(solution)/shard_map/all_to_all | solution.py:141
  188.6 366.1 %all-reduce.6 = bf16[128,4096]{1,0:T(8,128)(2,1)S(1)} all-reduce(f32[128,4096]{1,0:T(8,128)S(1)} %fusion.55), channel_id=2, replica_groups=mesh['oct'=2,'sub'=64] {'sub'}, use_global_device_ids=true, to_apply=%region_5.7.clone | all-reduce | flops 524288 | bytes 3145728
  559.8 8.0 reshape.324
  568.4 45.9 %all-gather.5.cloned.1.call-done = bf16[64,2,4096]{2,1,0:T(2,128)(2,1)} async-done(((bf16[1,2,4096]{2,1,0:T(2,128)(2,1)}), bf16[64,2,4096]{2,1,0:T(2,128)(2,1)}) %all-gather.5.cloned.1.call-update) | async-done | bytes 1048592 | tf_op jit(solution)/shard_map/all_gather | solution.py:163
  623.5 20.6 %convolution_convert_fusion = bf16[256,46080]{1,0:T(8,128)(2,1)} fusion(bf16[256,256]{1,0:T(8,128)(2,1)S(1)} %bitcast.222, bf16[256,46080]{1,0:T(8,128)(2,1)} %param.18), kind=kOutput, calls=%fused_computation.7 | convolution fusion | flops 6051594240 | bytes 47316992 | tf_op jit(solution)/shard_map/while/body/eval_jaxpr/dot_general | solution.py:101
  644.1 32.9 %reshape.327 = bf16[16,16,20,2304]{3,2,1,0:T(8,128)(2,1)} reshape(bf16[256,46080]{1,0:T(8,128)(2,1)} %convolution_convert_fusion) | data formatting | bytes 47185920 | tf_op jit(solution)/shard_map/while/body/eval_jaxpr/reshape | solution.py:106
  677.0 11.5 %convolution_bitcast_fusion = bf16[16,48,2304]{2,1,0:T(8,128)(2,1)S(1)} fusion(bf16[16,16,20,2304]{3,2,1,0:T(8,128)(2,1)} %reshape.327, bf16[20,48,16]{1,2,0:T(8,128)(2,1)} %param.17), kind=kOutput, calls=%fused_computation.11 | convolution fusion | flops 1132462080 | bytes 27162624 | tf_op jit(solution)/shard_map/while/body/eval_jaxpr/bxmr,max->bar/dot_general | solution.py:107
  688.6 5.1 reshape.328
  693.7 6.0 copy.55
  699.7 5.1 reshape.329
  704.8 8.5 gather_fusion.2
  716.8 5.3 scatter_custom_fusion.2
  726.8 36.1 %all_to_all.21 = bf16[128,2,4096]{2,1,0:T(2,128)(2,1)} all-to-all(bf16[128,2,4096]{2,1,0:T(2,128)(2,1)S(1)} %reshape.331), channel_id=1, replica_groups=mesh['oct'=2,'sub'=64] {'oct','sub'}, dimensions={0} | all-to-all | bytes 4194304 | tf_op jit(solution)/shard_map/all_to_all | solution.py:141
  772.7 130.4 %all-reduce.5.cloned.1.call-done = f32[128,4096]{1,0:T(8,128)} async-done(((f32[128,4096]{1,0:T(8,128)}), f32[128,4096]{1,0:T(8,128)}) %all-reduce.5.cloned.1.call-update) | async-done | bytes 2097168
  904.7 63.3 %all-gather.7.cloned.1.call-done = bf16[64,2,4096]{2,1,0:T(2,128)(2,1)} async-done(((bf16[1,2,4096]{2,1,0:T(2,128)(2,1)}), bf16[64,2,4096]{2,1,0:T(2,128)(2,1)}) %all-gather.7.cloned.1.call-update) | async-done | bytes 1048592 | tf_op jit(solution)/shard_map/all_gather | solution.py:163
  (182 shorter events, 95.0 us)
Async XLA Ops:
  10.2 16.2 %copy-start.32 = (s32[256,1]{0,1:T(1,128)}, s32[256,1]{0,1:T(1,128)S(1)}, u32[]{:S(2)}) copy-start(s32[256,1]{0,1:T(1,128)S(1)} %compare_select_fusion.1) | copy-start | bytes 3076
  13.1 127.0 %all-to-all-start = ((bf16[128,1,2]{2,1,0:T(2,128)(2,1)}), bf16[128,1,2]{2,1,0:T(2,128)(2,1)}, u32[]{:S(2)}, u32[]{:S(2)}) async-start(bf16[128,1,2]{2,1,0:T(2,128)(2,1)} %all_to_all.17), calls=%async_computation | async-start | bytes 131072 | tf_op jit(solution)/shard_map/all_to_all | solution.py:148
  27.1 98.5 %copy-start.21 = (pred[16,16]{1,0:T(8,128)(4,1)}, pred[16,16]{1,0:T(8,128)(4,1)S(1)}, u32[]{:S(2)}) copy-start(pred[16,16]{1,0:T(8,128)(4,1)S(1)} %and_bitcast_fusion) | copy-start | bytes 772
  34.2 21.4 %copy-start.6 = (f32[256,256,1]{1,0,2:T(8,128)}, f32[256,256,1]{1,0,2:T(8,128)S(1)}, u32[]{:S(2)}) copy-start(f32[256,256,1]{1,0,2:T(8,128)S(1)} %reshape.409) | copy-start | bytes 786436
  140.2 10.0 %copy-start.12 = (f32[2,16,16]{2,1,0:T(8,128)S(1)}, f32[2,16,16]{2,1,0:T(8,128)}, u32[]{:S(2)}) copy-start(f32[2,16,16]{2,1,0:T(8,128)} %param.19) | copy-start | bytes 6148
  140.2 39.8 %all-to-all-start.1 = ((bf16[128,2,4096]{2,1,0:T(2,128)(2,1)}), bf16[128,2,4096]{2,1,0:T(2,128)(2,1)S(1)}, u32[]{:S(2)}, u32[]{:S(2)}) async-start(bf16[128,2,4096]{2,1,0:T(2,128)(2,1)} %reshape.320), calls=%async_computation.1 | async-start | bytes 4194304 | tf_op jit(solution)/shard_map/all_to_all | solution.py:141
  150.1 464.2 %all-gather.5.cloned.1.call-start = ((), (), s32[]{:S(2)}) async-start(), calls=%async_computation.3 | async-start | bytes 1064960 | tf_op jit(solution)/shard_map/all_gather | solution.py:163
  154.6 10.3 %copy-start.35 = (u32[128]{0:T(128)S(1)}, u32[128]{0:T(128)}, u32[]{:S(2)}) copy-start(u32[128]{0:T(128)} %constant.167) | copy-start | bytes 1540
  154.6 11.7 %copy-start.34 = (s32[16]{0:T(128)S(1)}, s32[16]{0:T(128)}, u32[]{:S(2)}) copy-start(s32[16]{0:T(128)} %param.23) | copy-start | bytes 196
  154.6 11.7 %copy-start.33 = (s32[16]{0:T(128)S(1)}, s32[16]{0:T(128)}, u32[]{:S(2)}) copy-start(s32[16]{0:T(128)} %param.22) | copy-start | bytes 196
  164.9 19.3 %copy-start = (f32[1024,256]{1,0:T(8,128)}, f32[1024,256]{1,0:T(8,128)S(1)}, u32[]{:S(2)}) copy-start(f32[1024,256]{1,0:T(8,128)S(1)} %copy.78) | copy-start | bytes 3145732
  166.3 454.5 %copy-start.25 = (pred[16]{0:T(512)(128)(4,1)}, pred[16]{0:T(512)(128)(4,1)S(1)}, u32[]{:S(2)}) copy-start(pred[16]{0:T(512)(128)(4,1)S(1)} %fusion.85) | copy-start | bytes 52
  166.4 402.0 %copy-start.30 = (s32[16]{0:T(128)}, s32[16]{0:T(128)S(1)}, u32[]{:S(2)}) copy-start(s32[16]{0:T(128)S(1)} %get-tuple-element.37) | copy-start | bytes 196
  166.4 450.6 %copy-start.28 = (pred[16]{0:T(512)(128)(4,1)}, pred[16]{0:T(512)(128)(4,1)S(1)}, u32[]{:S(2)}) copy-start(pred[16]{0:T(512)(128)(4,1)S(1)} %get-tuple-element.36) | copy-start | bytes 52
  166.5 20.5 %copy-start.17 = (f32[16,16]{1,0:T(8,128)}, f32[16,16]{1,0:T(8,128)S(1)}, u32[]{:S(2)}) copy-start(f32[16,16]{1,0:T(8,128)S(1)} %get-tuple-element.48) | copy-start | bytes 3076
  166.5 20.5 %copy-start.19 = (f32[16,16]{1,0:T(8,128)}, f32[16,16]{1,0:T(8,128)S(1)}, u32[]{:S(2)}) copy-start(f32[16,16]{1,0:T(8,128)S(1)} %get-tuple-element.49) | copy-start | bytes 3076
  167.7 16.5 %copy-start.23 = (s32[256]{0:T(256)}, s32[256]{0:T(256)S(1)}, u32[]{:S(2)}) copy-start(s32[256]{0:T(256)S(1)} %reshape.335) | copy-start | bytes 3076
  555.3 347.8 %all-reduce.5.cloned.1.call-start = ((), (), s32[]{:S(2)}) async-start(), calls=%async_computation.5 | async-start | bytes 4194304
  568.2 49.9 %copy-start.2 = (f32[1024,256]{1,0:T(8,128)}, f32[1024,256]{1,0:T(8,128)S(1)}, u32[]{:S(2)}) copy-start(f32[1024,256]{1,0:T(8,128)S(1)} %copy.79) | copy-start | bytes 3145732
  568.3 52.6 %copy-start.13 = (f32[16,16]{1,0:T(8,128)}, f32[16,16]{1,0:T(8,128)S(1)}, u32[]{:S(2)}) copy-start(f32[16,16]{1,0:T(8,128)S(1)} %copy.45) | copy-start | bytes 3076
  568.3 52.5 %copy-start.15 = (f32[16,16]{1,0:T(8,128)}, f32[16,16]{1,0:T(8,128)S(1)}, u32[]{:S(2)}) copy-start(f32[16,16]{1,0:T(8,128)S(1)} %copy.46) | copy-start | bytes 3076
  568.4 48.6 %copy-start.27 = (s32[1024]{0:T(1024)}, s32[1024]{0:T(1024)S(1)}, u32[]{:S(2)}) copy-start(s32[1024]{0:T(1024)S(1)} %pad_clamp_fusion) | copy-start | bytes 12292
  772.6 195.3 %all-gather.7.cloned.1.call-start = ((), (), s32[]{:S(2)}) async-start(), calls=%async_computation.4 | async-start | bytes 1064960 | tf_op jit(solution)/shard_map/all_gather | solution.py:163
  904.7 66.5 %copy-start.29 = (pred[16]{0:T(512)(128)(4,1)S(1)}, pred[16]{0:T(512)(128)(4,1)}, u32[]{:S(2)}) copy-start(pred[16]{0:T(512)(128)(4,1)} %copy-done.28) | copy-start | bytes 52
  (17 other events, 51.6 us)
Sparse Core Ops, SparseCore 0:
  555.5 58.7 all-gather.4
  772.7 130.3 all-reduce.4
  906.6 61.3 all-gather.6
where the time goes:
time: 990 us; the launch traced here: 983 us
  blocking collectives  402 us (41%)
  waiting for transfers between devices  252 us (25%)
  local copies, waits for them, and re-layouts  180 us (18%)
  matrix products  85.5 us (9%)
  other arithmetic  26.4 us (3%)
  starting transfers between devices  21.9 us (2%)
  between operations  15.8 us (2%)
    unnamed x1, blocking collectives  366 us
    unnamed x4, waiting for transfers between devices  130 us
    all_gather x2, waiting for transfers between devices, shards(): lax.all_gather(own_parents.astype(jnp.bfloat16), 'sub', axis=0, tiled=True)  109 us
    reshape x2, local copies, waits for them, and re-layouts, convolve(): partial_value.reshape(block_boxes, order_k, term_count, 9 * plane_size)  65.8 us
    dot_general x2, matrix products, convolve(): jnp.dot(source_blk.reshape(block_boxes * order_k, plane_size), yz_kernels...  41.2 us
    all_to_all x1, blocking collectives, shards(): lax.all_to_all(send_tiles.reshape(devices_all, capacity, cube_size), ('oc...  36.1 us
    dot_general x2, matrix products, convolve(): jnp.einsum('bxmr,max->bar', partial_value, x_kernels, preferred_element_t...  23.1 us
  transfers between devices with their start and end apart: 5, of which 4 were waited for; matrix products, arithmetic and copies ran while one was open for 15% of the time, Pallas kernels for 0%

commit v1 on v0

v1 whole, which is shorter than its diff:
```python
import functools

import jax
import jax.numpy as jnp
from jax import lax
from jax.experimental import pallas as pl
from jax.experimental.pallas import tpu as pltpu
from jax.sharding import PartitionSpec as P

F32, BF16, I32 = jnp.float32, jnp.bfloat16, jnp.int32
K = 16
PLANE = K * K
BOXES = 16
ROWS = BOXES * K
TERMS = 20
SHIFTS = 9
LIST = 16
DEVICES = 128
GROUP = 64
CAP = 2
SLOTS = DEVICES * CAP
WIDE = SHIFTS * PLANE
VMEM_LIMIT = 66_000_000


def mm(a, b):
    return jnp.dot(a, b, preferred_element_type=F32)


def split(a):
    hi = a.astype(BF16)
    return hi, (a - hi.astype(F32)).astype(BF16)


def mm3(a, b):
    a_hi, a_lo = split(a)
    b_hi, b_lo = split(b)
    return mm(a_hi, b_hi) + (mm(a_hi, b_lo) + mm(a_lo, b_hi))


def exact(a, b):
    return jnp.dot(a, b, precision=lax.Precision.HIGHEST, preferred_element_type=F32)


def iotas(shape):
    return lax.broadcasted_iota(I32, shape, 0), lax.broadcasted_iota(I32, shape, 1)


def spreads():
    row, col = iotas((ROWS, K))
    high, low = (row // K == col).astype(F32), (row % K == col).astype(F32)
    row, col = iotas((K, ROWS))
    high_t, low_t = (col // K == row).astype(F32), (col % K == row).astype(F32)
    return high, low, high_t, low_t


def build_source(current, potential, table):
    high, low, high_t, low_t = spreads()
    row, col = iotas((ROWS, ROWS))
    table_t = table.T
    hh = exact(exact(high, table), high_t)
    ll = exact(exact(low, table), low_t)
    hh_t = exact(exact(high, table_t), high_t)
    ll_t = exact(exact(low, table_t), low_t)
    lh_t = exact(exact(low, table_t), high_t)
    left = jnp.where(row % K == col % K, hh, 0.0)
    left_back = jnp.where(row // K == col % K, lh_t, 0.0)
    values = mm3(left, mm3(current, hh_t * ll_t))
    product = values * (potential + 0.25 * values * values)
    return mm3(left_back, mm3(product, hh * ll)).astype(BF16)


def rows_of(ref):
    return jnp.concatenate([ref[:, x * PLANE : (x + 1) * PLANE] for x in range(K)], axis=0)


def start_yz(yz_hbm, yz_buf, sems):
    for m in range(TERMS):
        pltpu.make_async_copy(
            yz_hbm.at[:, m * WIDE : (m + 1) * WIDE], yz_buf.at[m], sems.at[m]
        ).start()


def convolve(source, xk_ref, yz_hbm, yz_buf, partial, conv, sems):
    def first(m, carry):
        pltpu.make_async_copy(yz_hbm.at[:, pl.ds(0, WIDE)], yz_buf.at[m], sems.at[m]).wait()
        at = pl.multiple_of(m * K, K)
        for p in range(SHIFTS):
            part = mm(source, yz_buf[m, :, p * PLANE : (p + 1) * PLANE])
            partial[p * BOXES : (p + 1) * BOXES, pl.ds(at, K), :] = part.astype(BF16).reshape(
                BOXES, K, PLANE
            )
        return carry

    lax.fori_loop(0, TERMS, first, 0)
    xk = xk_ref[...]

    def second(q, carry):
        out = mm(xk, partial[q])
        conv[pl.ds(q * 3, 3)] = out.astype(BF16).reshape(3, K, PLANE)
        return carry

    lax.fori_loop(0, SHIFTS * BOXES, second, 0, unroll=4)


def pick(conv, slot_ref, send_ref):
    def one(j, carry):
        send_ref[j] = conv[slot_ref[j]]
        return carry

    lax.fori_loop(0, SLOTS, one, 0, unroll=8)


def route(dest_ref, disp_ref, parent_ref, group_base, slot_ref, label_ref, up_ref, count):
    def clear(d, carry):
        count[d] = 0
        for c in range(CAP):
            slot_ref[d * CAP + c] = 0
            label_ref[d * CAP + c] = BOXES
        return carry

    lax.fori_loop(0, DEVICES, clear, 0)

    def clear_up(d, carry):
        up_ref[d] = 2 * BOXES
        return carry

    lax.fori_loop(0, GROUP, clear_up, 0)

    def one(j, carry):
        box, slot = j // LIST, j % LIST
        dest = dest_ref[box, slot]

        @pl.when(dest >= 0)
        def _():
            disp = disp_ref[box, slot]
            along_x = (disp * 57) // 512
            owner = dest // BOXES
            rank = count[owner]
            count[owner] = rank + 1
            slot_ref[owner * CAP + rank] = ((disp - SHIFTS * along_x) * BOXES + box) * 3 + along_x
            label_ref[owner * CAP + rank] = dest % BOXES

        return carry

    lax.fori_loop(0, BOXES * LIST, one, 0)

    def climb(box, carry):
        local = parent_ref[box] - group_base
        up_ref[local // 2] = box * 2 + local % 2
        return carry

    lax.fori_loop(0, BOXES, climb, 0)


def first_kernel(
    dest_ref, disp_ref, parent_ref, coef_ref, pot_ref, table_ref, xk_ref, yz_hbm,
    send_ref, slot_ref, label_ref, up_ref, yz_buf, partial, conv, count, sems,
):
    start_yz(yz_hbm, yz_buf, sems)
    route(
        dest_ref, disp_ref, parent_ref, (parent_ref[0] // 128) * 128,
        slot_ref, label_ref, up_ref, count,
    )
    source = build_source(rows_of(coef_ref), rows_of(pot_ref), table_ref[...])
    convolve(source, xk_ref, yz_hbm, yz_buf, partial, conv, sems)
    pick(conv, slot_ref, send_ref)


def octant_rows(octant_ref, order):
    row, col = iotas((ROWS, BOXES))
    hit = (row // K if order == "high" else row % K) == col
    return jnp.sum(jnp.where(hit, octant_ref[...], 0), axis=1, keepdims=True)


def by_octant(blocks, octants, half, high_filters, low_filters):
    out = jnp.zeros((ROWS, PLANE), F32)
    for c in range(4):
        quad = (high_filters[c // 2] * low_filters[c % 2]).astype(BF16)
        out = jnp.where(octants % 4 == c, mm(blocks, quad), out)
    return out


def gather_kernel(label_ref, up_ref, recv_ref, scale_ref, octant_ref, gathered_ref, up_send, acc, lifted):
    acc[...] = jnp.zeros_like(acc)

    def one(j, carry):
        c = label_ref[j]
        acc[c] = acc[c] + recv_ref[j].astype(F32)
        return carry

    lax.fori_loop(0, SLOTS, one, 0, unroll=8)
    gathered = acc[:BOXES].reshape(ROWS, PLANE)
    gathered_ref[...] = gathered
    high, low, high_t, low_t = spreads()
    row, col = iotas((ROWS, ROWS))
    filters_t = [scale_ref[c].T for c in range(2)]
    high_filters = [exact(exact(high, f), high_t) for f in filters_t]
    low_filters = [exact(exact(low, f), low_t) for f in filters_t]
    octants = octant_rows(octant_ref, "high")
    inner = by_octant(gathered.astype(BF16), octants, PLANE, high_filters, low_filters)
    lefts = [exact(exact(low, scale_ref[c]), low_t) for c in range(2)]
    left = jnp.where(octants // 4 == 1, lefts[1], lefts[0])
    left = jnp.where(row // K == col // K, left, 0.0)
    out = mm(left.astype(BF16), inner.astype(BF16))
    lifted[...] = out.astype(BF16).reshape(BOXES, K, PLANE)

    def send(d, carry):
        up_send[d] = lifted[jnp.minimum(up_ref[d] // 2, BOXES - 1)]
        return carry

    lax.fori_loop(0, GROUP, send, 0, unroll=8)


def parent_kernel(up_label_ref, recv_ref, parents_ref, down_ref, acc, rounded):
    acc[...] = jnp.zeros_like(acc)

    def one(d, carry):
        p = up_label_ref[d]
        acc[p] = acc[p] + recv_ref[d].astype(F32)
        return carry

    lax.fori_loop(0, GROUP, one, 0, unroll=8)
    for p in range(2):
        for i in range(K):
            parents_ref[p : p + 1, i * PLANE : (i + 1) * PLANE] = acc[p, i : i + 1, :]
    rounded[...] = acc[:2].astype(BF16)

    def send(d, carry):
        down_ref[d] = rounded[jnp.minimum(up_label_ref[d], 1)]
        return carry

    lax.fori_loop(0, GROUP, send, 0, unroll=8)


def corrected(parent_ref, down_ref, gathered_ref, scale_ref, octant_ref, matched):
    group_base = (parent_ref[0] // 128) * 128

    def one(b, carry):
        matched[b] = down_ref[(parent_ref[b] - group_base) // 2]
        return carry

    lax.fori_loop(0, BOXES, one, 0, unroll=4)
    high, low, high_t, low_t = spreads()
    row, col = iotas((ROWS, ROWS))
    high_filters = [exact(exact(high, scale_ref[c]), high_t) for c in range(2)]
    low_filters = [exact(exact(low, scale_ref[c]), low_t) for c in range(2)]
    octants = octant_rows(octant_ref, "high")
    inner = by_octant(
        matched[...].reshape(ROWS, PLANE), octants, PLANE, high_filters, low_filters
    )
    lefts = [exact(exact(high, scale_ref[c].T), low_t) for c in range(2)]
    left = jnp.where(octant_rows(octant_ref, "low") // 4 == 1, lefts[1], lefts[0])
    same = row % K == col // K
    left = jnp.where(same, left, 0.0)
    swap = jnp.where(same & (row // K == col % K), 1.0, 0.0).astype(BF16)
    g_hi, g_lo = split(gathered_ref[...])
    return mm(swap, g_hi) + mm(swap, g_lo) - mm(left.astype(BF16), inner.astype(BF16))


def again_kernel(
    slot_ref, parent_ref, down_ref, gathered_ref, scale_ref, octant_ref, pot_ref, table_ref, xk_ref, yz_hbm,
    send_ref, yz_buf, partial, conv, matched, sems,
):
    start_yz(yz_hbm, yz_buf, sems)
    current = corrected(parent_ref, down_ref, gathered_ref, scale_ref, octant_ref, matched)
    source = build_source(current, rows_of(pot_ref), table_ref[...])
    convolve(source, xk_ref, yz_hbm, yz_buf, partial, conv, sems)
    pick(conv, slot_ref, send_ref)


def last_kernel(parent_ref, down_ref, gathered_ref, scale_ref, octant_ref, out_ref, matched):
    current = corrected(parent_ref, down_ref, gathered_ref, scale_ref, octant_ref, matched)
    for x in range(K):
        out_ref[:, x * PLANE : (x + 1) * PLANE] = current[x * BOXES : (x + 1) * BOXES, :]


SMEM = pl.BlockSpec(memory_space=pltpu.SMEM)
VMEM = pl.BlockSpec(memory_space=pltpu.VMEM)
ANY = pl.BlockSpec(memory_space=pl.ANY)


def call(kernel, outs, out_specs, in_specs, scratch, *args, limit=None):
    return pl.pallas_call(
        kernel,
        out_shape=outs,
        in_specs=in_specs,
        out_specs=out_specs,
        scratch_shapes=scratch,
        compiler_params=pltpu.CompilerParams(vmem_limit_bytes=limit),
    )(*args)


def tiles(count, kind=BF16):
    return jax.ShapeDtypeStruct((count, K, PLANE), kind)


def ints(count):
    return jax.ShapeDtypeStruct((count,), I32)


def shards(
    coefficients,
    potential,
    to_values,
    x_kernels,
    yz_kernels,
    two_scale,
    disp_ids,
    dest_box,
    parent_of,
    child_octant,
):
    xk = x_kernels.transpose(1, 0, 2).reshape(3 * K, TERMS * K)
    octant = child_octant.reshape(1, BOXES)
    heavy = [
        pltpu.VMEM((TERMS, PLANE, WIDE), BF16),
        pltpu.VMEM((SHIFTS * BOXES, TERMS * K, PLANE), BF16),
        pltpu.VMEM((SHIFTS * BOXES * 3, K, PLANE), BF16),
    ]
    everyone = ("oct", "sub")
    swap = functools.partial(lax.all_to_all, split_axis=0, concat_axis=0, tiled=True)
    send, slots, labels, ups = call(
        first_kernel,
        (tiles(SLOTS), ints(SLOTS), ints(SLOTS), ints(GROUP)),
        (VMEM, SMEM, SMEM, SMEM),
        [SMEM] * 3 + [VMEM] * 4 + [ANY],
        heavy + [pltpu.SMEM((DEVICES,), I32), pltpu.SemaphoreType.DMA((TERMS,))],
        dest_box, disp_ids, parent_of, coefficients, potential, to_values, xk, yz_kernels,
        limit=VMEM_LIMIT,
    )
    up_out = jnp.where(ups >= 2 * BOXES, 2, ups % 2)
    box_labels = swap(labels.astype(BF16).reshape(DEVICES, CAP), everyone).reshape(-1).astype(I32)
    up_labels = swap(up_out.astype(BF16).reshape(GROUP, 1), "sub").reshape(-1).astype(I32)
    for iteration in range(2):
        recv = swap(send, everyone)
        gathered, up_send = call(
            gather_kernel,
            (jax.ShapeDtypeStruct((ROWS, PLANE), F32), tiles(GROUP)),
            (VMEM, VMEM),
            [SMEM, SMEM, VMEM, VMEM, VMEM],
            [pltpu.VMEM((BOXES + 1, K, PLANE), F32), pltpu.VMEM((BOXES, K, PLANE), BF16)],
            box_labels, ups, recv, two_scale, octant,
        )
        up_recv = swap(up_send, "sub")
        parents, down_send = call(
            parent_kernel,
            (jax.ShapeDtypeStruct((2, K * PLANE), F32), tiles(GROUP)),
            (VMEM, VMEM),
            [SMEM, VMEM],
            [pltpu.VMEM((3, K, PLANE), F32), pltpu.VMEM((2, K, PLANE), BF16)],
            up_labels, up_recv,
        )
        down_recv = swap(down_send, "sub")
        matched = pltpu.VMEM((BOXES, K, PLANE), BF16)
        if iteration == 0:
            send = call(
                again_kernel,
                tiles(SLOTS),
                VMEM,
                [SMEM] * 2 + [VMEM] * 7 + [ANY],
                heavy + [matched, pltpu.SemaphoreType.DMA((TERMS,))],
                slots, parent_of, down_recv, gathered, two_scale, octant, potential, to_values, xk, yz_kernels,
                limit=VMEM_LIMIT,
            )
        else:
            field = call(
                last_kernel,
                jax.ShapeDtypeStruct((BOXES, K * PLANE), F32),
                VMEM,
                [SMEM] + [VMEM] * 4,
                [matched],
                parent_of, down_recv, gathered, two_scale, octant,
            )
    return field, parents


def solution(mesh):
    spread = P(("oct", "sub"), None)
    placed = (spread, spread, P(), P(), P(), P(), spread, spread, P(("oct", "sub")), P(("oct", "sub")))
    return jax.shard_map(
        shards, mesh=mesh, in_specs=placed, out_specs=(spread, spread), check_vma=False
    )
```

time: 990 us -> 264 us (0.27)
  blocking collectives: 402 us -> 110 us
  waiting for transfers between devices: 252 us -> 40.7 us
  local copies, waits for them, and re-layouts: 180 us -> 4.01 us
  Pallas kernels: 0 us -> 86 us
  matrix products: 85.5 us -> 0 us
  other arithmetic: 26.4 us -> 2.62 us
  between operations: 15.8 us -> 0.71 us
    unnamed x1 -> x0, blocking collectives: 366 us -> none
    unnamed x4 -> x0, waiting for transfers between devices: 130 us -> none
    reshape x18 -> x1, local copies, waits for them, and re-layouts: 121 us -> 1.58 us  [shards(): xk = x_kernels.transpose(1, 0, 2).reshape(3 * K, TERMS * K)]
    all_gather x2 -> x0, waiting for transfers between devices: 109 us -> none  [shards(): lax.all_gather(own_parents.astype(jnp.bfloat16), 'sub', axis=0, tiled=True)]
    pallas_call x0 -> x7, Pallas kernels: none -> 86 us  [call(): pl.pallas_call(kernel, out_shape=outs, in_specs=in_specs, out_specs=out_s...]
    dot_general x28 -> x0, matrix products: 85.5 us -> none  [the longest x2 41.2 us: convolve(): jnp.dot(source_blk.reshape(block_boxes * order_k, plane_size), yz_kernels...]
    all_to_all x1 -> x5, blocking collectives: 36.1 us -> 110 us  [the longest x1 35.7 us: shards(): recv = swap(send, everyone)]
    all_to_all x2 -> x3, waiting for transfers between devices: 12.3 us -> 40.7 us  [the longest x1 28.2 us: shards(): recv = swap(send, everyone)]
  transfers between devices with their start and end apart: 5 -> 3, of which waited for: 4 -> 3; matrix products, arithmetic and copies ran while one was open for 15% -> 1% of each run, Pallas kernels for 0% -> 3%
where the time goes in v1:
time: 264 us; the launch traced here: 263 us
  blocking collectives  110 us (42%)
  Pallas kernels  86 us (33%)
  waiting for transfers between devices  40.7 us (15%)
  starting transfers between devices  19.8 us (8%)
  local copies, waits for them, and re-layouts  4.01 us (2%)
    pallas_call x7, Pallas kernels, call(): pl.pallas_call(kernel, out_shape=outs, in_specs=in_specs, out_specs=out_s...  86 us
    all_to_all x1, blocking collectives, shards(): recv = swap(send, everyone)  35.7 us
    all_to_all x2, blocking collectives, shards(): down_recv = swap(down_send, 'sub')  34.3 us
    all_to_all x1, waiting for transfers between devices, shards(): recv = swap(send, everyone)  28.2 us
    all_to_all x1, blocking collectives, shards(): swap(labels.astype(BF16).reshape(DEVICES, CAP), everyone).reshape(-1)  20.1 us
    all_to_all x1, blocking collectives, shards(): up_recv = swap(up_send, 'sub')  19.3 us
    all_to_all x1, waiting for transfers between devices, shards(): up_recv = swap(up_send, 'sub')  10.5 us
    all_to_all x1, starting transfers between devices, shards(): up_recv = swap(up_send, 'sub')  8.31 us
  transfers between devices with their start and end apart: 3, of which 3 were waited for; matrix products, arithmetic and copies ran while one was open for 1% of the time, Pallas kernels for 3%

profile of v1, /device:TPU:0, one launch (start us, length us, event | category | flops | bytes accessed | tf_op | source)
XLA Modules:
  0.0 263.3 jit_solution(15843861304411719003)
XLA Ops:
  0.6 1.6 copy.19.xk_ref
  2.2 33.4 %shard_map.113 = (bf16[256,16,256]{2,1,0:T(8,128)(2,1)}, s32[256]{0:T(256)}, s32[256]{0:T(256)}, s32[64]{0:T(128)}) custom-call(s32[16,16]{1,0:T(8,128)} %dest_ref.1, s32[16,16]{1,0:T(8,128)} %disp_ref.1, s32[16]{0:T(128)} %parent_ref.5, f32[16,4096]{1,0:T(8,128)} %coef_ref.1, f32[16,4096]{1,0:T(8,128)} %pot_ref.3, f32[16,16]{1,0:T(8,128)} %table_ref.3, ...), custom_call_target="tpu_custom_call" | custom-call | tf_op jit(solution)/shard_map/pallas_call | solution.py:284
  35.6 0.7 convert_element_type.19
  36.5 20.1 %all_to_all.49 = bf16[128,1,2]{2,1,0:T(2,128)(2,1)S(1)} all-to-all(bf16[128,1,2]{2,1,0:T(2,128)(2,1)S(1)} %all_to_all.40), channel_id=1, replica_groups=mesh['oct'=2,'sub'=64] {'oct','sub'}, dimensions={0} | all-to-all | bytes 1024 | tf_op jit(solution)/shard_map/all_to_all | solution.py:333
  56.6 4.9 %all-to-all-start.2 = ((bf16[256,16,256]{2,1,0:T(8,128)(2,1)}), bf16[256,16,256]{2,1,0:T(8,128)(2,1)S(1)}, u32[]{:S(2)}, u32[]{:S(2)}) async-start(bf16[256,16,256]{2,1,0:T(8,128)(2,1)} %get-tuple-element.16), calls=%async_computation.2 | async-start | bytes 4194304 | tf_op jit(solution)/shard_map/all_to_all | solution.py:336
  61.5 0.7 copy.20
  62.5 0.7 reshape.29.label_ref
  63.2 28.2 %all-to-all-done.2.recv_ref = bf16[256,16,256]{2,1,0:T(8,128)(2,1)S(1)} async-done(((bf16[256,16,256]{2,1,0:T(8,128)(2,1)}), bf16[256,16,256]{2,1,0:T(8,128)(2,1)S(1)}, u32[]{:S(2)}, u32[]{:S(2)}) %all-to-all-start.2) | async-done | bytes 2097184 | tf_op jit(solution)/shard_map/all_to_all | solution.py:336
  91.4 6.6 %all-to-all-start = ((bf16[64,1,1]{2,1,0:T(2,128)(2,1)}), bf16[64,1,1]{2,1,0:T(2,128)(2,1)S(1)}, u32[]{:S(2)}, u32[]{:S(2)}) async-start(bf16[64,1,1]{2,1,0:T(2,128)(2,1)} %copy.20), calls=%async_computation | async-start | bytes 65536 | tf_op jit(solution)/shard_map/all_to_all | solution.py:334
  98.0 7.5 %shard_map.114 = (f32[256,256]{1,0:T(8,128)}, bf16[64,16,256]{2,1,0:T(8,128)(2,1)}) custom-call(s32[256]{0:T(256)} %reshape.29.label_ref, s32[64]{0:T(128)} %get-tuple-element.13.up_ref, bf16[256,16,256]{2,1,0:T(8,128)(2,1)} %copy-done, f32[2,16,16]{2,1,0:T(8,128)} %scale_ref.7, s32[1,16]{1,0:T(1,128)} %bitcast.7), custom_call_target="tpu_custom_call" | custom-call | tf_op jit(solution)/shard_map/pallas_call | solution.py:284
  105.5 2.0 all-to-all-done
  107.5 8.3 %all-to-all-start.3 = ((bf16[64,16,256]{2,1,0:T(8,128)(2,1)}), bf16[64,16,256]{2,1,0:T(8,128)(2,1)S(1)}, u32[]{:S(2)}, u32[]{:S(2)}) async-start(bf16[64,16,256]{2,1,0:T(8,128)(2,1)} %get-tuple-element.17), calls=%async_computation.3 | async-start | bytes 1048576 | tf_op jit(solution)/shard_map/all_to_all | solution.py:345
  115.8 1.7 convert_reduce_fusion.1.up_label_ref
  117.5 10.5 %all-to-all-done.3.recv_ref = bf16[64,16,256]{2,1,0:T(8,128)(2,1)S(1)} async-done(((bf16[64,16,256]{2,1,0:T(8,128)(2,1)}), bf16[64,16,256]{2,1,0:T(8,128)(2,1)S(1)}, u32[]{:S(2)}, u32[]{:S(2)}) %all-to-all-start.3) | async-done | bytes 524320 | tf_op jit(solution)/shard_map/all_to_all | solution.py:345
  128.1 0.8 copy-done.1
  128.9 2.4 shard_map.115
  131.3 17.1 %all_to_all.50.down_ref = bf16[64,16,256]{2,1,0:T(8,128)(2,1)} all-to-all(bf16[64,16,256]{2,1,0:T(8,128)(2,1)} %get-tuple-element.18), channel_id=1, replica_groups=mesh['oct'=2,'sub'=64] {'sub'}, dimensions={0} | all-to-all | bytes 1048576 | tf_op jit(solution)/shard_map/all_to_all | solution.py:354
  148.4 27.6 %shard_map.116 = bf16[256,16,256]{2,1,0:T(8,128)(2,1)} custom-call(s32[256]{0:T(256)} %get-tuple-element.15.slot_ref, s32[16]{0:T(128)} %parent_ref.5, bf16[64,16,256]{2,1,0:T(8,128)(2,1)} %all_to_all.50.down_ref, f32[256,256]{1,0:T(8,128)} %get-tuple-element.19.gathered_ref, f32[2,16,16]{2,1,0:T(8,128)} %scale_ref.7, s32[1,16]{1,0:T(1,128)} %bitcast.8, ...), custom_call_target="tpu_custom_call" | custom-call | tf_op jit(solution)/shard_map/pallas_call | solution.py:284
  176.0 35.7 %all_to_all.51.recv_ref = bf16[256,16,256]{2,1,0:T(8,128)(2,1)} all-to-all(bf16[256,16,256]{2,1,0:T(8,128)(2,1)} %shard_map.116), channel_id=1, replica_groups=mesh['oct'=2,'sub'=64] {'oct','sub'}, dimensions={0} | all-to-all | bytes 4194304 | tf_op jit(solution)/shard_map/all_to_all | solution.py:336
  211.7 7.5 %shard_map.117 = (f32[256,256]{1,0:T(8,128)}, bf16[64,16,256]{2,1,0:T(8,128)(2,1)}) custom-call(s32[256]{0:T(256)} %reshape.29.label_ref, s32[64]{0:T(128)} %get-tuple-element.13.up_ref, bf16[256,16,256]{2,1,0:T(8,128)(2,1)} %all_to_all.51.recv_ref, f32[2,16,16]{2,1,0:T(8,128)} %scale_ref.7, s32[1,16]{1,0:T(1,128)} %bitcast.9), custom_call_target="tpu_custom_call" | custom-call | tf_op jit(solution)/shard_map/pallas_call | solution.py:284
  219.2 19.3 %all_to_all.52.recv_ref = bf16[64,16,256]{2,1,0:T(8,128)(2,1)} all-to-all(bf16[64,16,256]{2,1,0:T(8,128)(2,1)} %get-tuple-element.20), channel_id=1, replica_groups=mesh['oct'=2,'sub'=64] {'sub'}, dimensions={0} | all-to-all | bytes 1048576 | tf_op jit(solution)/shard_map/all_to_all | solution.py:345
  238.5 2.4 shard_map.118
  240.9 17.2 %all_to_all.53.down_ref = bf16[64,16,256]{2,1,0:T(8,128)(2,1)} all-to-all(bf16[64,16,256]{2,1,0:T(8,128)(2,1)} %get-tuple-element.21), channel_id=1, replica_groups=mesh['oct'=2,'sub'=64] {'sub'}, dimensions={0} | all-to-all | bytes 1048576 | tf_op jit(solution)/shard_map/all_to_all | solution.py:354
  258.2 5.2 %shard_map.119 = f32[16,4096]{1,0:T(8,128)} custom-call(s32[16]{0:T(128)} %parent_ref.5, bf16[64,16,256]{2,1,0:T(8,128)(2,1)} %all_to_all.53.down_ref, f32[256,256]{1,0:T(8,128)} %get-tuple-element.22.gathered_ref, f32[2,16,16]{2,1,0:T(8,128)} %scale_ref.7, s32[1,16]{1,0:T(1,128)} %bitcast.10), custom_call_target="tpu_custom_call" | custom-call | tf_op jit(solution)/shard_map/pallas_call | solution.py:284
  (8 shorter events, 0.4 us)
Async XLA Ops:
  56.6 4.9 %copy-start.2 = (s32[64]{0:T(128)S(1)}, s32[64]{0:T(128)}, u32[]{:S(2)}) copy-start(s32[64]{0:T(128)} %get-tuple-element.13.up_ref) | copy-start | bytes 772
  56.6 34.8 %all-to-all-start.2 = ((bf16[256,16,256]{2,1,0:T(8,128)(2,1)}), bf16[256,16,256]{2,1,0:T(8,128)(2,1)S(1)}, u32[]{:S(2)}, u32[]{:S(2)}) async-start(bf16[256,16,256]{2,1,0:T(8,128)(2,1)} %get-tuple-element.16), calls=%async_computation.2 | async-start | bytes 4194304 | tf_op jit(solution)/shard_map/all_to_all | solution.py:336
  91.4 6.6 %copy-start = (bf16[256,16,256]{2,1,0:T(8,128)(2,1)}, bf16[256,16,256]{2,1,0:T(8,128)(2,1)S(1)}, u32[]{:S(2)}) copy-start(bf16[256,16,256]{2,1,0:T(8,128)(2,1)S(1)} %all-to-all-done.2.recv_ref) | copy-start | bytes 6291460
  91.4 16.1 %all-to-all-start = ((bf16[64,1,1]{2,1,0:T(2,128)(2,1)}), bf16[64,1,1]{2,1,0:T(2,128)(2,1)S(1)}, u32[]{:S(2)}, u32[]{:S(2)}) async-start(bf16[64,1,1]{2,1,0:T(2,128)(2,1)} %copy.20), calls=%async_computation | async-start | bytes 65536 | tf_op jit(solution)/shard_map/all_to_all | solution.py:334
  107.5 20.6 %all-to-all-start.3 = ((bf16[64,16,256]{2,1,0:T(8,128)(2,1)}), bf16[64,16,256]{2,1,0:T(8,128)(2,1)S(1)}, u32[]{:S(2)}, u32[]{:S(2)}) async-start(bf16[64,16,256]{2,1,0:T(8,128)(2,1)} %get-tuple-element.17), calls=%async_computation.3 | async-start | bytes 1048576 | tf_op jit(solution)/shard_map/all_to_all | solution.py:345
  128.1 0.8 copy-start.1

commit v2 on v1

v2 whole, which is shorter than its diff:
```python
import functools

import jax
import jax.numpy as jnp
from jax import lax
from jax.experimental import pallas as pl
from jax.experimental.pallas import tpu as pltpu
from jax.sharding import PartitionSpec as P

F32, BF16, I32 = jnp.float32, jnp.bfloat16, jnp.int32
MESH = pl.DeviceIdType.MESH
ITERS = 2
K = 16
PLANE = K * K
BOXES = 16
ROWS = BOXES * K
TERMS = 20
SHIFTS = 9
LIST = 16
DEVICES = 128
GROUP = 64
CAP = 2
SLOTS = DEVICES * CAP
WIDE = SHIFTS * PLANE
SIDE = 4
STRIDE, UNSTRIDE = 37, 45
BURST = 4
BATCH = 8
UP_BATCH = 16
NO_PARENT = 2
VMEM_LIMIT = 67_000_000


def mm(a, b):
    return jnp.dot(a, b, preferred_element_type=F32)


def split(a):
    hi = a.astype(BF16)
    return hi, (a - hi.astype(F32)).astype(BF16)


def mm3(a, b):
    return mm(a[0], b[0]) + (mm(a[0], b[1]) + mm(a[1], b[0]))


def exact(a, b):
    return jnp.dot(a, b, precision=lax.Precision.HIGHEST, preferred_element_type=F32)


def iotas(shape):
    return lax.broadcasted_iota(I32, shape, 0), lax.broadcasted_iota(I32, shape, 1)


def spreads():
    row, col = iotas((ROWS, K))
    high, low = (row // K == col).astype(F32), (row % K == col).astype(F32)
    row, col = iotas((K, ROWS))
    high_t, low_t = (col // K == row).astype(F32), (col % K == row).astype(F32)
    return high, low, high_t, low_t


def fill_values(table, mats):
    high, low, high_t, low_t = spreads()
    row, col = iotas((ROWS, ROWS))
    table_t = table.T
    hh = exact(exact(high, table), high_t)
    ll = exact(exact(low, table), low_t)
    hh_t = exact(exact(high, table_t), high_t)
    ll_t = exact(exact(low, table_t), low_t)
    lh_t = exact(exact(low, table_t), high_t)
    left = jnp.where(row % K == col % K, hh, 0.0)
    left_back = jnp.where(row // K == col % K, lh_t, 0.0)
    for n, mat in enumerate((left, hh_t * ll_t, left_back, hh * ll)):
        hi, lo = split(mat)
        mats[2 * n] = hi
        mats[2 * n + 1] = lo


def octant_rows(octant_ref, digit):
    row, col = iotas((ROWS, BOXES))
    hit = (row // K if digit == "high" else row % K) == col
    return jnp.sum(jnp.where(hit, octant_ref[...], 0), axis=1, keepdims=True)


def fill_tree(scale_ref, octant_ref, up_mats, down_mats, sides):
    high, low, high_t, low_t = spreads()
    row, col = iotas((ROWS, ROWS))
    filters = [scale_ref[c] for c in range(2)]
    turned = [f.T for f in filters]
    for mats, pair in ((up_mats, turned), (down_mats, filters)):
        highs = [exact(exact(high, f), high_t) for f in pair]
        lows = [exact(exact(low, f), low_t) for f in pair]
        for c in range(4):
            mats[c] = (highs[c // 2] * lows[c % 2]).astype(BF16)
    ups = [exact(exact(low, f), low_t) for f in filters]
    up = jnp.where(octant_rows(octant_ref, "high") // 4 == 1, ups[1], ups[0])
    sides[0] = jnp.where(row // K == col // K, up, 0.0).astype(BF16)
    downs = [exact(exact(high, f), low_t) for f in turned]
    down = jnp.where(octant_rows(octant_ref, "low") // 4 == 1, downs[1], downs[0])
    same = row % K == col // K
    sides[1] = jnp.where(same, down, 0.0).astype(BF16)
    sides[2] = jnp.where(same & (row // K == col % K), 1.0, 0.0).astype(BF16)


def by_octant(blocks, octants, mats):
    out = mm(blocks, mats[0])
    for c in range(1, 4):
        out = jnp.where(octants == c, mm(blocks, mats[c]), out)
    return out


def source_of(current, pot_ref, mats):
    pairs = [(mats[2 * n], mats[2 * n + 1]) for n in range(4)]
    values = mm3(pairs[0], split(mm3(split(current), pairs[1])))
    product = values * (rows_of(pot_ref) + 0.25 * values * values)
    return mm3(pairs[2], split(mm3(split(product), pairs[3]))).astype(BF16)


def rows_of(ref):
    return jnp.concatenate([ref[:, x * PLANE : (x + 1) * PLANE] for x in range(K)], axis=0)


def place():
    sub = lax.axis_index("sub")
    return lax.axis_index("oct"), sub // (SIDE * SIDE), (sub // SIDE) % SIDE, sub % SIDE


def partner(order, sign):
    core, x, z, y = place()
    k = lax.rem((order // 2) * STRIDE, GROUP)
    step = GROUP if sign < 0 else 0
    x = lax.rem(x + sign * (k // 16) + step, SIDE)
    z = lax.rem(z + sign * lax.rem(k // SIDE, SIDE) + step, SIDE)
    y = lax.rem(y + sign * lax.rem(k, SIDE) + step, SIDE)
    return (lax.rem(core + lax.rem(order, 2), 2), (x * SIDE + z) * SIDE + y)


def route_kernel(
    me_ref, dest_ref, disp_ref, parent_ref, plane_ref, shift_ref, child_ref, home_ref, labels_ref, count, label, up,
):
    core, sub = me_ref[0], me_ref[1]
    x, z, y = sub // 16, (sub // SIDE) % SIDE, sub % SIDE

    def order_of(other_core, other):
        kx = lax.rem(other // 16 - x + SIDE, SIDE)
        kz = lax.rem(lax.rem(other // SIDE, SIDE) - z + SIDE, SIDE)
        ky = lax.rem(lax.rem(other, SIDE) - y + SIDE, SIDE)
        u = lax.rem(((kx * SIDE + kz) * SIDE + ky) * UNSTRIDE, GROUP)
        return 2 * u + lax.rem(other_core - core + 2, 2)

    def clear(d, carry):
        count[d] = 0
        up[d] = NO_PARENT
        for c in range(CAP):
            plane_ref[d * CAP + c] = 0
            shift_ref[d * CAP + c] = 0
            label[d * CAP + c] = BOXES
        return carry

    lax.fori_loop(0, DEVICES, clear, 0)

    def clear_child(d, carry):
        child_ref[d] = 0
        return carry

    lax.fori_loop(0, GROUP, clear_child, 0)

    def one(j, carry):
        box, slot = j // LIST, lax.rem(j, LIST)
        dest = dest_ref[box, slot]

        @pl.when(dest >= 0)
        def _():
            disp = disp_ref[box, slot]
            along_x = (disp * 57) // 512
            order = order_of(dest // (BOXES * GROUP), lax.rem(dest // BOXES, GROUP))
            rank = count[order]
            count[order] = rank + 1
            at = order * CAP + rank
            plane_ref[at] = (disp - SHIFTS * along_x) * BOXES + box
            shift_ref[at] = along_x
            label[at] = lax.rem(dest, BOXES)

        return carry

    lax.fori_loop(0, BOXES * LIST, one, 0)

    def climb(box, carry):
        parent = lax.rem(parent_ref[box], 2 * GROUP)
        order = order_of(core, parent // 2)
        up[order] = lax.rem(parent, 2)
        child_ref[order // 2] = box
        home_ref[box] = order // 2
        return carry

    lax.fori_loop(0, BOXES, climb, 0)
    first = (lax.broadcasted_iota(I32, (1, PLANE), 1) // K) % 2 == 0

    def row(d, carry):
        both = jnp.where(first, label[d * CAP], label[d * CAP + 1])
        labels_ref[d] = both + 32 * up[d]
        return carry

    lax.fori_loop(0, DEVICES, row, 0, unroll=8)


def main_kernel(
    plane_ref, shift_ref, child_ref, home_ref,
    labels_ref, coef_ref, pot_ref, table_ref, scale_ref, octant_ref, xk_ref, yz_hbm,
    field_ref, parents_ref,
    yz_buf, partial, send, recv, up_send, up_recv, down_send, down_recv, tags,
    mats, up_mats, down_mats, sides, lifted, matched,
    yz_sem, tag_sem, send_sem, recv_sem, tree_sem,
):
    for m in range(TERMS):
        pltpu.make_async_copy(
            yz_hbm.at[:, m * WIDE : (m + 1) * WIDE], yz_buf.at[m], yz_sem.at[m]
        ).start()
    barrier = pltpu.get_barrier_semaphore()

    def greet(j, carry):
        pl.semaphore_signal(barrier, inc=1, device_id=partner(j, 1), device_id_type=MESH)
        return carry

    lax.fori_loop(1, DEVICES, greet, 0)

    def remote(source, target, out_sem, in_sem, device):
        return pltpu.make_async_remote_copy(
            src_ref=source, dst_ref=target, send_sem=out_sem, recv_sem=in_sem,
            device_id=device, device_id_type=MESH,
        )

    def arrived(region, out_sem, in_sem):
        remote(region, region, out_sem, in_sem, partner(1, 1)).wait_recv()

    def left(region, out_sem, in_sem):
        remote(region, region, out_sem, in_sem, partner(1, 1)).wait_send()

    fill_values(table_ref[...], mats)
    source = source_of(rows_of(coef_ref), pot_ref, mats)
    fill_tree(scale_ref, octant_ref, up_mats, down_mats, sides)
    octants = octant_rows(octant_ref, "high") % 4
    row, col = iotas((ROWS, ROWS))
    same_plane = row % K == col % K
    row_box = row // K

    for it in range(ITERS):

        def first(m, carry, it=it, source=source):
            if it == 0:
                pltpu.make_async_copy(
                    yz_hbm.at[:, pl.ds(0, WIDE)], yz_buf.at[m], yz_sem.at[m]
                ).wait()
            at = pl.multiple_of(m * K, K)
            for p in range(SHIFTS):
                part = mm(source, yz_buf[m, :, p * PLANE : (p + 1) * PLANE])
                partial[p * BOXES : (p + 1) * BOXES, pl.ds(at, K), :] = part.astype(BF16).reshape(
                    BOXES, K, PLANE
                )
            return carry

        lax.fori_loop(0, TERMS, first, 0)

        if it == 0:
            pl.semaphore_wait(barrier, DEVICES - 1)

            def tell(j, carry):
                remote(labels_ref.at[j], tags.at[j], tag_sem.at[0], tag_sem.at[1], partner(j, 1)).start()
                return carry

            lax.fori_loop(1, DEVICES, tell, 0)
            tags[0] = labels_ref[0]
        else:
            left(send.at[pl.ds(1, DEVICES - 1)], send_sem.at[it - 1], recv_sem.at[0, 0])

        def ship(j, it=it):
            batch = j // BATCH
            return remote(
                send.at[j], recv.at[it, j], send_sem.at[it], recv_sem.at[it, batch], partner(j, 1)
            )

        def burst(n, carry, it=it, ship=ship):
            for e in range(BURST):
                before = (n - 1) * BURST + e

                @pl.when(before >= 1)
                def _():
                    ship(before).start()

            for e in range(BURST):
                for c in range(CAP):
                    at = (n * BURST + e) * CAP + c
                    tile = mm(xk_ref[shift_ref[at]], partial[plane_ref[at]])
                    send[n * BURST + e, c] = tile.astype(BF16)
            return carry

        bursts = DEVICES // BURST
        lax.fori_loop(0, bursts, burst, 0)
        for e in range(BURST):
            ship((bursts - 1) * BURST + e).start()
        recv[it, 0] = send[0]

        if it == 0:
            arrived(tags.at[pl.ds(1, DEVICES - 1)], tag_sem.at[0], tag_sem.at[1])

        gathered = jnp.zeros((ROWS, PLANE), F32)
        for g in range(DEVICES // BATCH):
            lo = max(1, g * BATCH)
            arrived(
                recv.at[it, pl.ds(lo, (g + 1) * BATCH - lo)], send_sem.at[it], recv_sem.at[it, g]
            )
            marks = tags[g * BATCH : (g + 1) * BATCH].reshape(BATCH, PLANE) % 32
            row8, col8 = iotas((BATCH, PLANE))
            marks = jnp.sum(
                jnp.where(row8 == col8 // (CAP * K), marks, 0), axis=0, keepdims=True
            )
            member = jnp.where(same_plane & (marks == row_box), 1.0, 0.0).astype(BF16)
            block = recv[it, g * BATCH : (g + 1) * BATCH].reshape(ROWS, PLANE)
            gathered = gathered + mm(member, block)

        inner = by_octant(gathered.astype(BF16), octants, up_mats)
        up = mm(sides[0], inner.astype(BF16))
        lifted[...] = up.astype(BF16).reshape(BOXES, K, PLANE)

        def fill_up(u, carry):
            up_send[u] = lifted[child_ref[u]]
            return carry

        if it > 0:
            left(up_send.at[pl.ds(1, GROUP - 1)], tree_sem.at[it - 1, 0], tree_sem.at[0, 1])
        lax.fori_loop(0, GROUP, fill_up, 0, unroll=8)

        def ship_up(u, carry, it=it):
            remote(
                up_send.at[u], up_recv.at[it, u], tree_sem.at[it, 0], tree_sem.at[it, 1],
                partner(2 * u, 1),
            ).start()
            return carry

        lax.fori_loop(1, GROUP, ship_up, 0)
        up_recv[it, 0] = up_send[0]
        arrived(up_recv.at[it, pl.ds(1, GROUP - 1)], tree_sem.at[it, 0], tree_sem.at[it, 1])

        sums = jnp.zeros((2 * K, PLANE), F32)
        row_p, col_p = iotas((2 * K, PLANE))
        for h in range(GROUP // UP_BATCH):
            span = 2 * UP_BATCH
            marks = tags[h * span : (h + 1) * span].reshape(span, PLANE) // 32
            row_s, col_s = iotas((span, PLANE))
            marks = jnp.sum(jnp.where(row_s == 2 * (col_s // K), marks, 0), axis=0, keepdims=True)
            member = jnp.where((row_p % K == col_p % K) & (marks == row_p // K), 1.0, 0.0)
            block = up_recv[it, h * UP_BATCH : (h + 1) * UP_BATCH].reshape(ROWS, PLANE)
            sums = sums + mm(member.astype(BF16), block)
        if it == ITERS - 1:
            for p in range(2):
                for i in range(K):
                    at = p * K + i
                    parents_ref[p : p + 1, i * PLANE : (i + 1) * PLANE] = sums[at : at + 1, :]

        if it > 0:
            left(down_send.at[pl.ds(1, GROUP - 1)], tree_sem.at[it - 1, 2], tree_sem.at[0, 3])

        def fill_down(u, carry, sums=sums):
            second = tags[2 * u] // 32 == 1
            down_send[u] = jnp.where(second, sums[K:], sums[:K]).astype(BF16)
            return carry

        lax.fori_loop(0, GROUP, fill_down, 0, unroll=8)

        def ship_down(u, carry, it=it):
            remote(
                down_send.at[u], down_recv.at[it, u], tree_sem.at[it, 2], tree_sem.at[it, 3],
                partner(2 * u, -1),
            ).start()
            return carry

        lax.fori_loop(1, GROUP, ship_down, 0)
        down_recv[it, 0] = down_send[0]
        arrived(down_recv.at[it, pl.ds(1, GROUP - 1)], tree_sem.at[it, 2], tree_sem.at[it, 3])

        for b in range(BOXES):
            matched[b] = down_recv[it, home_ref[b]]
        inner = by_octant(matched[...].reshape(ROWS, PLANE), octants, down_mats)
        g_hi, g_lo = split(gathered)
        current = mm(sides[2], g_hi) + mm(sides[2], g_lo) - mm(sides[1], inner.astype(BF16))
        if it < ITERS - 1:
            source = source_of(current, pot_ref, mats)
        else:
            for x in range(K):
                field_ref[:, x * PLANE : (x + 1) * PLANE] = current[x * BOXES : (x + 1) * BOXES, :]

    last = ITERS - 1
    left(tags.at[pl.ds(1, DEVICES - 1)], tag_sem.at[0], tag_sem.at[1])
    left(send.at[pl.ds(1, DEVICES - 1)], send_sem.at[last], recv_sem.at[0, 0])
    left(up_send.at[pl.ds(1, GROUP - 1)], tree_sem.at[last, 0], tree_sem.at[0, 1])
    left(down_send.at[pl.ds(1, GROUP - 1)], tree_sem.at[last, 2], tree_sem.at[0, 3])


SMEM = pl.BlockSpec(memory_space=pltpu.SMEM)
VMEM = pl.BlockSpec(memory_space=pltpu.VMEM)
ANY = pl.BlockSpec(memory_space=pl.ANY)


def shards(
    coefficients,
    potential,
    to_values,
    x_kernels,
    yz_kernels,
    two_scale,
    disp_ids,
    dest_box,
    parent_of,
    child_octant,
):
    xk = x_kernels.transpose(1, 0, 2).reshape(3, K, TERMS * K)
    octant = child_octant.reshape(1, BOXES)
    me = jnp.stack([lax.axis_index("oct"), lax.axis_index("sub")]).astype(I32)
    ints = functools.partial(jax.ShapeDtypeStruct, dtype=I32)
    planes, shifts, children, homes, labels = pl.pallas_call(
        route_kernel,
        out_shape=(ints((SLOTS,)), ints((SLOTS,)), ints((GROUP,)), ints((BOXES,)), ints((DEVICES, 1, PLANE))),
        in_specs=[SMEM] * 4,
        out_specs=(SMEM, SMEM, SMEM, SMEM, VMEM),
        scratch_shapes=[
            pltpu.SMEM((DEVICES,), I32),
            pltpu.SMEM((SLOTS,), I32),
            pltpu.SMEM((DEVICES,), I32),
        ],
    )(me, dest_box, disp_ids, parent_of)
    mat = (ROWS, ROWS)
    dma = pltpu.SemaphoreType.DMA
    return pl.pallas_call(
        main_kernel,
        out_shape=(
            jax.ShapeDtypeStruct((BOXES, K * PLANE), F32),
            jax.ShapeDtypeStruct((2, K * PLANE), F32),
        ),
        in_specs=[SMEM] * 4 + [VMEM] * 7 + [ANY],
        out_specs=(VMEM, VMEM),
        scratch_shapes=[
            pltpu.VMEM((TERMS, PLANE, WIDE), BF16),
            pltpu.VMEM((SHIFTS * BOXES, TERMS * K, PLANE), BF16),
            pltpu.VMEM((DEVICES, CAP, K, PLANE), BF16),
            pltpu.VMEM((ITERS, DEVICES, CAP, K, PLANE), BF16),
            pltpu.VMEM((GROUP, K, PLANE), BF16),
            pltpu.VMEM((ITERS, GROUP, K, PLANE), BF16),
            pltpu.VMEM((GROUP, K, PLANE), BF16),
            pltpu.VMEM((ITERS, GROUP, K, PLANE), BF16),
            pltpu.VMEM((DEVICES, 1, PLANE), I32),
            pltpu.VMEM((8, *mat), BF16),
            pltpu.VMEM((4, *mat), BF16),
            pltpu.VMEM((4, *mat), BF16),
            pltpu.VMEM((3, *mat), BF16),
            pltpu.VMEM((BOXES, K, PLANE), BF16),
            pltpu.VMEM((BOXES, K, PLANE), BF16),
            dma((TERMS,)),
            dma((2,)),
            dma((ITERS,)),
            dma((ITERS, DEVICES // BATCH)),
            dma((ITERS, 4)),
        ],
        compiler_params=pltpu.CompilerParams(
            vmem_limit_bytes=VMEM_LIMIT, collective_id=0, has_side_effects=True
        ),
    )(
        planes, shifts, children, homes,
        labels, coefficients, potential, to_values, two_scale, octant, xk, yz_kernels,
    )


def solution(mesh):
    spread = P(("oct", "sub"), None)
    placed = (spread, spread, P(), P(), P(), P(), spread, spread, P(("oct", "sub")), P(("oct", "sub")))
    return jax.shard_map(
        shards, mesh=mesh, in_specs=placed, out_specs=(spread, spread), check_vma=False
    )
```

time: 264 us -> 168 us (0.64)
  blocking collectives: 110 us -> 0 us
  Pallas kernels: 86 us -> 161 us
  waiting for transfers between devices: 40.7 us -> 0 us
  starting transfers between devices: 19.8 us -> 0 us
    all_to_all x5 -> x0, blocking collectives: 110 us -> none  [the longest x1 35.7 us: shards(): recv = swap(send, everyone)]
    pallas_call x7 -> x2, Pallas kernels: 86 us -> 161 us  [the longest x1 144 us: shards(): pl.pallas_call(main_kernel, out_shape=(jax.ShapeDtypeStruct((BOXES, K * P...]
    all_to_all x3 -> x0, waiting for transfers between devices: 40.7 us -> none  [the longest x1 28.2 us: shards(): recv = swap(send, everyone)]
    all_to_all x3 -> x0, starting transfers between devices: 19.8 us -> none  [the longest x1 8.31 us: shards(): up_recv = swap(up_send, 'sub')]
  transfers between devices with their start and end apart: 3 -> 0, of which waited for: 3 -> 0; matrix products, arithmetic and copies ran while one was open for 1% -> 0% of each run, Pallas kernels for 3% -> 0%
where the time goes in v2:
time: 168 us; the launch traced here: 167 us
  Pallas kernels  161 us (96%)
  local copies, waits for them, and re-layouts  4.89 us (3%)
    pallas_call x1, Pallas kernels, shards(): pl.pallas_call(main_kernel, out_shape=(jax.ShapeDtypeStruct((BOXES, K * P...  144 us
    pallas_call x1, Pallas kernels, shards(): pl.pallas_call(route_kernel, out_shape=(ints((SLOTS,)), ints((SLOTS,)), i...  16.7 us

profile of v2, /device:TPU:0, one launch (start us, length us, event | category | flops | bytes accessed | tf_op | source)
XLA Modules:
  0.0 167.3 jit_solution(971947494988961142)
XLA Ops:
  0.6 0.6 pad_add_fusion.me_ref
  1.2 16.7 %shard_map.113 = (s32[256]{0:T(256)}, s32[256]{0:T(256)}, s32[64]{0:T(128)}, s32[16]{0:T(128)}, s32[128,1,256]{2,1,0:T(1,128)}) custom-call(s32[2]{0:T(128)} %pad_add_fusion.me_ref, s32[16,16]{1,0:T(8,128)} %dest_ref.1, s32[16,16]{1,0:T(8,128)} %disp_ref.1, s32[16]{0:T(128)} %parent_ref.1), custom_call_target="tpu_custom_call" | custom-call | tf_op jit(solution)/shard_map/pallas_call | solution.py:421
  17.9 1.0 reshape.12
  19.0 0.8 copy.14.xk_ref
  19.8 144.4 %shard_map.114 = (f32[16,4096]{1,0:T(8,128)}, f32[2,4096]{1,0:T(2,128)}) custom-call(s32[256]{0:T(256)} %get-tuple-element.7.plane_ref, s32[256]{0:T(256)} %get-tuple-element.8.shift_ref, s32[64]{0:T(128)} %get-tuple-element.9.child_ref, s32[16]{0:T(128)} %get-tuple-element.10.home_ref, s32[128,1,256]{2,1,0:T(1,128)} %get-tuple-element.11.labels_ref, ...), custom_call_target="tpu_custom_call" | custom-call | tf_op jit(solution)/shard_map/pallas_call | solution.py:434
  164.2 1.7 copy.17
  165.9 1.4 copy.18

commit v3 on v2

v3 whole, which is shorter than its diff:
```python
import functools

import jax
import jax.numpy as jnp
from jax import lax
from jax.experimental import pallas as pl
from jax.experimental.pallas import tpu as pltpu
from jax.sharding import PartitionSpec as P

F32, BF16, I32 = jnp.float32, jnp.bfloat16, jnp.int32
MESH = pl.DeviceIdType.MESH
ITERS = 2
K = 16
PLANE = K * K
BOXES = 16
ROWS = BOXES * K
TERMS = 20
SHIFTS = 9
LIST = 16
DEVICES = 128
GROUP = 64
CAP = 2
HALVES, HALF = 2, PLANE // 2
SLOTS = DEVICES * CAP
WIDE = SHIFTS * PLANE
SIDE = 4
BURSTS = GROUP // SIDE
BATCH = DEVICES // BURSTS
UP_BATCH = 16
NO_PARENT = 2
CHILD, HOME, TABLE = 2 * SLOTS, 2 * SLOTS + DEVICES, 2 * SLOTS + 2 * DEVICES
VMEM_LIMIT = 67_000_000


def mm(a, b):
    return jnp.dot(a, b, preferred_element_type=F32)


def split(a):
    hi = a.astype(BF16)
    return hi, (a - hi.astype(F32)).astype(BF16)


def mm3(a, b):
    return mm(a[0], b[0]) + (mm(a[0], b[1]) + mm(a[1], b[0]))


def exact(a, b):
    return jnp.dot(a, b, precision=lax.Precision.HIGHEST, preferred_element_type=F32)


def iotas(shape):
    return lax.broadcasted_iota(I32, shape, 0), lax.broadcasted_iota(I32, shape, 1)


def spreads():
    row, col = iotas((ROWS, K))
    high, low = (row // K == col).astype(F32), (row % K == col).astype(F32)
    row, col = iotas((K, ROWS))
    high_t, low_t = (col // K == row).astype(F32), (col % K == row).astype(F32)
    return high, low, high_t, low_t


def fill_values(table, mats):
    high, low, high_t, low_t = spreads()
    row, col = iotas((ROWS, ROWS))
    table_t = table.T
    hh = exact(exact(high, table), high_t)
    ll = exact(exact(low, table), low_t)
    hh_t = exact(exact(high, table_t), high_t)
    ll_t = exact(exact(low, table_t), low_t)
    lh_t = exact(exact(low, table_t), high_t)
    left = jnp.where(row % K == col % K, hh, 0.0)
    left_back = jnp.where(row // K == col % K, lh_t, 0.0)
    for n, mat in enumerate((left, hh_t * ll_t, left_back, hh * ll)):
        hi, lo = split(mat)
        mats[2 * n] = hi
        mats[2 * n + 1] = lo


def octant_rows(octant_ref, digit):
    row, col = iotas((ROWS, BOXES))
    hit = (row // K if digit == "high" else row % K) == col
    return jnp.sum(jnp.where(hit, octant_ref[...], 0), axis=1, keepdims=True)


def fill_tree(scale_ref, octant_ref, up_mats, down_mats, sides):
    high, low, high_t, low_t = spreads()
    row, col = iotas((ROWS, ROWS))
    filters = [scale_ref[c] for c in range(2)]
    turned = [f.T for f in filters]
    for mats, pair in ((up_mats, turned), (down_mats, filters)):
        highs = [exact(exact(high, f), high_t) for f in pair]
        lows = [exact(exact(low, f), low_t) for f in pair]
        for c in range(4):
            mats[c] = (highs[c // 2] * lows[c % 2]).astype(BF16)
    ups = [exact(exact(low, f), low_t) for f in filters]
    up = jnp.where(octant_rows(octant_ref, "high") // 4 == 1, ups[1], ups[0])
    sides[0] = jnp.where(row // K == col // K, up, 0.0).astype(BF16)
    downs = [exact(exact(high, f), low_t) for f in turned]
    down = jnp.where(octant_rows(octant_ref, "low") // 4 == 1, downs[1], downs[0])
    same = row % K == col // K
    sides[1] = jnp.where(same, down, 0.0).astype(BF16)
    sides[2] = jnp.where(same & (row // K == col % K), 1.0, 0.0).astype(BF16)


def by_octant(blocks, octants, mats):
    out = mm(blocks, mats[0])
    for c in range(1, 4):
        out = jnp.where(octants == c, mm(blocks, mats[c]), out)
    return out


def source_of(current, pot_ref, mats):
    pairs = [(mats[2 * n], mats[2 * n + 1]) for n in range(4)]
    values = mm3(pairs[0], split(mm3(split(current), pairs[1])))
    product = values * (rows_of(pot_ref) + 0.25 * values * values)
    return mm3(pairs[2], split(mm3(split(product), pairs[3]))).astype(BF16)


def rows_of(ref):
    return jnp.concatenate([ref[:, x * PLANE : (x + 1) * PLANE] for x in range(K)], axis=0)


def place():
    sub = lax.axis_index("sub")
    return lax.axis_index("oct"), sub // (SIDE * SIDE), (sub // SIDE) % SIDE, sub % SIDE


def burst_of(n, sign):
    core, x, z, y = place()
    a, kz = n // SIDE, lax.rem(n, SIDE)
    z_part = lax.rem(z + sign * kz + SIDE, SIDE) * SIDE
    chips = []
    for ky in range(SIDE):
        x_part = lax.rem(x + sign * (a + kz + ky) + 3 * SIDE, SIDE) * (SIDE * SIDE)
        chips.append(x_part + z_part + lax.rem(y + sign * ky + SIDE, SIDE))
    cores = (core, 1 - core)
    return [[(cores[c], chips[t]) for c in range(2)] for t in range(SIDE)]


def in_bursts(ship, fill=None):
    if fill is None:
        ship(0, 1)

        def step(n, carry):
            ship(n, 0)
            return carry

        lax.fori_loop(1, BURSTS, step, 0)
        return
    fill(0)
    ship(0, 1)
    fill(1)

    def step(n, carry):
        ship(n - 1, 0)
        fill(n)
        return carry

    lax.fori_loop(2, BURSTS, step, 0)
    ship(BURSTS - 1, 0)


def displacement_order(own, core, sub):
    core_0, x, z, y = own
    kx, kz, ky = (sub // 16 - x) & 3, (sub // SIDE - z) & 3, (sub - y) & 3
    u = (((kx - kz - ky) & 3) * SIDE + kz) * SIDE + ky
    return 2 * u + ((core - core_0) & 1)


def whole(a):
    return (a + 1.5).astype(I32) - 1


def route_kernel(dest_ref, disp_ref, parent_ref, table_ref, labels_ref):
    own = place()
    high, low, high_t, low_t = spreads()
    count = BOXES * LIST

    def as_row(v):
        spread = exact(v.astype(F32), low_t)
        return whole(jnp.sum(jnp.where(high_t > 0.5, spread, 0.0), axis=0, keepdims=True))

    def as_col(v):
        spread = exact(high, v.astype(F32))
        return whole(jnp.sum(jnp.where(low > 0.5, spread, 0.0), axis=1, keepdims=True))

    row, col = iotas((count, count))

    def order_of(dest):
        block = dest >> 4
        order = displacement_order(own, block >> 6, block & (GROUP - 1))
        return jnp.where(dest >= 0, order, -1)

    dest_row, dest_col, disp_col = as_row(dest_ref[...]), as_col(dest_ref[...]), as_col(disp_ref[...])
    order_row, order_col = order_of(dest_row), order_of(dest_col)
    same = order_row == order_col
    rank_row = jnp.sum(jnp.where(same & (row < col), 1, 0), axis=0, keepdims=True)
    rank_col = jnp.sum(jnp.where(same & (col < row), 1, 0), axis=1, keepdims=True)
    at_row = jnp.where(order_row >= 0, order_row * CAP + rank_row, -1)
    at_col = jnp.where(order_col >= 0, order_col * CAP + rank_col, -1)
    along_x = (disp_col * 57) >> 9
    box_col = lax.broadcasted_iota(I32, (count, 1), 0) // LIST
    plane_col = (disp_col - SHIFTS * along_x) * BOXES + box_col
    hit = at_col == col
    table_ref[:, :SLOTS] = jnp.sum(jnp.where(hit, plane_col, 0), axis=0, keepdims=True)
    table_ref[:, SLOTS : 2 * SLOTS] = jnp.sum(jnp.where(hit, along_x, 0), axis=0, keepdims=True)

    parent_row = parent_ref[...] & (2 * GROUP - 1)
    up_row = displacement_order(own, own[0], parent_row >> 1)
    row_b, col_b = iotas((BOXES, BOXES))
    up_col = jnp.sum(jnp.where(row_b == col_b, up_row, 0), axis=1, keepdims=True)
    row_u, col_u = iotas((BOXES, DEVICES))
    children = jnp.sum(jnp.where(up_col == 2 * col_u, row_u, 0), axis=0, keepdims=True)
    table_ref[:, CHILD:HOME] = children
    table_ref[:, HOME : HOME + BOXES] = up_row >> 1

    order, lane = iotas((DEVICES, count))
    which = (dest_row & (BOXES - 1)) - BOXES
    labels = [
        jnp.sum(jnp.where(at_row == order * CAP + c, which, 0), axis=1, keepdims=True) + BOXES
        for c in range(CAP)
    ]
    order_b, lane_b = iotas((DEVICES, BOXES))
    ups = jnp.sum(
        jnp.where(up_row == order_b, (parent_row & 1) - NO_PARENT, 0), axis=1, keepdims=True
    )
    marks = jnp.where((lane // K) % CAP == 0, labels[0], labels[1]) + 32 * (ups + NO_PARENT)
    labels_ref[...] = marks.reshape(DEVICES, 1, PLANE)


def main_kernel(
    slots_ref, labels_ref, coef_ref, pot_ref, table_ref, scale_ref, octant_ref, xk_ref, yz_hbm,
    field_ref, parents_ref,
    yz_buf, partial, send, recv, up_send, up_recv, down_send, down_recv, tags,
    mats, up_mats, down_mats, sides, lifted, matched, xk,
    yz_sem, tag_sem, send_sem, recv_sem, tree_sem,
):
    for m in range(TERMS):
        pltpu.make_async_copy(
            yz_hbm.at[:, m * WIDE : (m + 1) * WIDE], yz_buf.at[m], yz_sem.at[m]
        ).start()
    barrier = pltpu.get_barrier_semaphore()
    someone = burst_of(jnp.int32(0), 1)[1][0]

    def greet(n, skip):
        devices = burst_of(jnp.int32(n), 1)
        for e in range(skip, BATCH):
            pl.semaphore_signal(
                barrier, inc=1, device_id=devices[e // 2][e % 2], device_id_type=MESH
            )

    in_bursts(greet)

    def remote(source, target, out_sem, in_sem, device):
        return pltpu.make_async_remote_copy(
            src_ref=source, dst_ref=target, send_sem=out_sem, recv_sem=in_sem,
            device_id=device, device_id_type=MESH,
        )

    def arrived(region, out_sem, in_sem):
        remote(region, region, out_sem, in_sem, someone).wait_recv()

    def left(region, out_sem, in_sem):
        remote(region, region, out_sem, in_sem, someone).wait_send()

    xk[...] = xk_ref[...].astype(F32).T.astype(BF16).reshape(3, K, TERMS * K)
    fill_values(table_ref[...], mats)
    source = source_of(rows_of(coef_ref), pot_ref, mats)
    octants = octant_rows(octant_ref, "high") % 4
    row, col = iotas((ROWS, ROWS))
    same_plane = row % K == col % K
    row_box = row // K

    pl.semaphore_wait(barrier, DEVICES - 1)

    def tell(n, skip):
        devices = burst_of(jnp.int32(n), 1)
        for e in range(skip, BATCH):
            j = n * BATCH + e
            remote(
                labels_ref.at[j], tags.at[j], tag_sem.at[0], tag_sem.at[1], devices[e // 2][e % 2]
            ).start()

    tell(0, 1)
    tags[0] = labels_ref[0]

    for it in range(ITERS):

        if it > 0:
            left(send.at[:, pl.ds(1, DEVICES - 1)], send_sem.at[it - 1], recv_sem.at[0, 0, 0])
        for h in range(HALVES):
            lanes = slice(h * HALF, (h + 1) * HALF)

            def product(pair, it=it, source=source, h=h, lanes=lanes):
                if it == 0 and h == 0:
                    for e in range(2):
                        m = 2 * pair + e
                        pltpu.make_async_copy(
                            yz_hbm.at[:, pl.ds(0, WIDE)], yz_buf.at[m], yz_sem.at[m]
                        ).wait()
                at = pl.multiple_of(pair * 2 * K, 2 * K)
                for p in range(SHIFTS):
                    lo = p * PLANE + h * HALF
                    both = jnp.concatenate(
                        [yz_buf[2 * pair + e, :, lo : lo + HALF] for e in range(2)], axis=1
                    )
                    part = mm(source, both).astype(BF16)
                    for e in range(2):
                        partial[p * BOXES : (p + 1) * BOXES, pl.ds(at + e * K, K), lanes] = part[
                            :, e * HALF : (e + 1) * HALF
                        ].reshape(BOXES, K, HALF)

            def step(pair, carry, product=product):
                product(pair)
                return carry

            def telling(pair, carry, product=product):
                for e in range(3):
                    tell(1 + 3 * pair + e, 0)
                product(pair)
                return carry

            if it == 0 and h == 0:
                lax.fori_loop(0, BURSTS // 3, telling, 0)
                lax.fori_loop(BURSTS // 3, TERMS // 2, step, 0)
            else:
                lax.fori_loop(0, TERMS // 2, step, 0)

            def ship(n, skip, it=it, h=h):
                devices = burst_of(jnp.int32(n), 1)
                for e in range(skip, BATCH):
                    j = n * BATCH + e
                    remote(
                        send.at[h, j], recv.at[it, h, j], send_sem.at[it], recv_sem.at[it, h, n],
                        devices[e // 2][e % 2],
                    ).start()

            def fill(n, h=h, lanes=lanes):
                for e in range(BATCH):
                    j = n * BATCH + e
                    at = [j * CAP + c for c in range(CAP)]
                    factors = jnp.concatenate([xk[slots_ref[0, SLOTS + i]] for i in at], axis=0)
                    parts = jnp.concatenate([partial[slots_ref[0, i], :, lanes] for i in at], axis=1)
                    both = mm(factors, parts).astype(BF16)
                    for c in range(CAP):
                        send[h, j, c] = both[c * K : (c + 1) * K, c * HALF : (c + 1) * HALF]

            in_bursts(ship, fill)
            recv[it, h, 0] = send[h, 0]

        if it == 0:
            fill_tree(scale_ref, octant_ref, up_mats, down_mats, sides)
        if it == 0:
            arrived(tags.at[pl.ds(1, DEVICES - 1)], tag_sem.at[0], tag_sem.at[1])

        halves = []
        for h in range(HALVES):
            total = jnp.zeros((ROWS, HALF), F32)
            for g in range(BURSTS):
                lo = max(1, g * BATCH)
                arrived(
                    recv.at[it, h, pl.ds(lo, (g + 1) * BATCH - lo)],
                    send_sem.at[it], recv_sem.at[it, h, g],
                )
                marks = tags[g * BATCH : (g + 1) * BATCH].reshape(BATCH, PLANE) % 32
                row8, col8 = iotas((BATCH, PLANE))
                marks = jnp.sum(
                    jnp.where(row8 == col8 // (CAP * K), marks, 0), axis=0, keepdims=True
                )
                member = jnp.where(same_plane & (marks == row_box), 1.0, 0.0).astype(BF16)
                block = recv[it, h, g * BATCH : (g + 1) * BATCH].reshape(ROWS, HALF)
                total = total + mm(member, block)
            halves.append(total)
        gathered = jnp.concatenate(halves, axis=1)

        inner = by_octant(gathered.astype(BF16), octants, up_mats)
        up = mm(sides[0], inner.astype(BF16))
        lifted[...] = up.astype(BF16).reshape(BOXES, K, PLANE)

        if it > 0:
            left(up_send.at[pl.ds(1, GROUP - 1)], tree_sem.at[it - 1, 0], tree_sem.at[0, 1])

        def ship_up(n, skip, it=it):
            devices = burst_of(jnp.int32(n), 1)
            for t in range(skip, SIDE):
                u = n * SIDE + t
                remote(
                    up_send.at[u], up_recv.at[it, u], tree_sem.at[it, 0], tree_sem.at[it, 1],
                    devices[t][0],
                ).start()

        def fill_up(n):
            for t in range(SIDE):
                up_send[n * SIDE + t] = lifted[slots_ref[0, CHILD + n * SIDE + t]]

        in_bursts(ship_up, fill_up)
        up_recv[it, 0] = up_send[0]
        arrived(up_recv.at[it, pl.ds(1, GROUP - 1)], tree_sem.at[it, 0], tree_sem.at[it, 1])

        sums = jnp.zeros((2 * K, PLANE), F32)
        row_p, col_p = iotas((2 * K, PLANE))
        for h in range(GROUP // UP_BATCH):
            span = 2 * UP_BATCH
            marks = tags[h * span : (h + 1) * span].reshape(span, PLANE) // 32
            row_s, col_s = iotas((span, PLANE))
            marks = jnp.sum(jnp.where(row_s == 2 * (col_s // K), marks, 0), axis=0, keepdims=True)
            member = jnp.where((row_p % K == col_p % K) & (marks == row_p // K), 1.0, 0.0)
            block = up_recv[it, h * UP_BATCH : (h + 1) * UP_BATCH].reshape(ROWS, PLANE)
            sums = sums + mm(member.astype(BF16), block)
        if it == ITERS - 1:
            for p in range(2):
                for i in range(K):
                    at = p * K + i
                    parents_ref[p : p + 1, i * PLANE : (i + 1) * PLANE] = sums[at : at + 1, :]

        if it > 0:
            left(down_send.at[pl.ds(1, GROUP - 1)], tree_sem.at[it - 1, 2], tree_sem.at[0, 3])

        def ship_down(n, skip, it=it):
            devices = burst_of(jnp.int32(n), -1)
            for t in range(skip, SIDE):
                u = n * SIDE + t
                remote(
                    down_send.at[u], down_recv.at[it, u], tree_sem.at[it, 2], tree_sem.at[it, 3],
                    devices[t][0],
                ).start()

        def fill_down(n, sums=sums):
            for t in range(SIDE):
                second = tags[2 * (n * SIDE + t)] // 32 == 1
                down_send[n * SIDE + t] = jnp.where(second, sums[K:], sums[:K]).astype(BF16)

        in_bursts(ship_down, fill_down)
        down_recv[it, 0] = down_send[0]
        arrived(down_recv.at[it, pl.ds(1, GROUP - 1)], tree_sem.at[it, 2], tree_sem.at[it, 3])

        for b in range(BOXES):
            matched[b] = down_recv[it, slots_ref[0, HOME + b]]
        inner = by_octant(matched[...].reshape(ROWS, PLANE), octants, down_mats)
        g_hi, g_lo = split(gathered)
        current = mm(sides[2], g_hi) + mm(sides[2], g_lo) - mm(sides[1], inner.astype(BF16))
        if it < ITERS - 1:
            source = source_of(current, pot_ref, mats)
        else:
            for x in range(K):
                field_ref[:, x * PLANE : (x + 1) * PLANE] = current[x * BOXES : (x + 1) * BOXES, :]

    last = ITERS - 1
    left(tags.at[pl.ds(1, DEVICES - 1)], tag_sem.at[0], tag_sem.at[1])
    left(send.at[:, pl.ds(1, DEVICES - 1)], send_sem.at[last], recv_sem.at[0, 0, 0])
    left(up_send.at[pl.ds(1, GROUP - 1)], tree_sem.at[last, 0], tree_sem.at[0, 1])
    left(down_send.at[pl.ds(1, GROUP - 1)], tree_sem.at[last, 2], tree_sem.at[0, 3])


SMEM = pl.BlockSpec(memory_space=pltpu.SMEM)
VMEM = pl.BlockSpec(memory_space=pltpu.VMEM)
ANY = pl.BlockSpec(memory_space=pl.ANY)


def shards(
    coefficients,
    potential,
    to_values,
    x_kernels,
    yz_kernels,
    two_scale,
    disp_ids,
    dest_box,
    parent_of,
    child_octant,
):
    xk = x_kernels.transpose(0, 2, 1).reshape(TERMS * K, 3 * K)
    octant = child_octant.reshape(1, BOXES)
    ints = functools.partial(jax.ShapeDtypeStruct, dtype=I32)
    slots, labels = pl.pallas_call(
        route_kernel,
        out_shape=(ints((1, TABLE)), ints((DEVICES, 1, PLANE))),
        in_specs=[VMEM] * 3,
        out_specs=(VMEM, VMEM),
    )(dest_box, disp_ids, parent_of.reshape(1, BOXES))
    mat = (ROWS, ROWS)
    dma = pltpu.SemaphoreType.DMA
    return pl.pallas_call(
        main_kernel,
        out_shape=(
            jax.ShapeDtypeStruct((BOXES, K * PLANE), F32),
            jax.ShapeDtypeStruct((2, K * PLANE), F32),
        ),
        in_specs=[SMEM] + [VMEM] * 7 + [ANY],
        out_specs=(VMEM, VMEM),
        scratch_shapes=[
            pltpu.VMEM((TERMS, PLANE, WIDE), BF16),
            pltpu.VMEM((SHIFTS * BOXES, TERMS * K, PLANE), BF16),
            pltpu.VMEM((HALVES, DEVICES, CAP, K, HALF), BF16),
            pltpu.VMEM((ITERS, HALVES, DEVICES, CAP, K, HALF), BF16),
            pltpu.VMEM((GROUP, K, PLANE), BF16),
            pltpu.VMEM((ITERS, GROUP, K, PLANE), BF16),
            pltpu.VMEM((GROUP, K, PLANE), BF16),
            pltpu.VMEM((ITERS, GROUP, K, PLANE), BF16),
            pltpu.VMEM((DEVICES, 1, PLANE), I32),
            pltpu.VMEM((8, *mat), BF16),
            pltpu.VMEM((4, *mat), BF16),
            pltpu.VMEM((4, *mat), BF16),
            pltpu.VMEM((3, *mat), BF16),
            pltpu.VMEM((BOXES, K, PLANE), BF16),
            pltpu.VMEM((BOXES, K, PLANE), BF16),
            pltpu.VMEM((3, K, TERMS * K), BF16),
            dma((TERMS,)),
            dma((2,)),
            dma((ITERS,)),
            dma((ITERS, HALVES, BURSTS)),
            dma((ITERS, 4)),
        ],
        compiler_params=pltpu.CompilerParams(
            vmem_limit_bytes=VMEM_LIMIT, collective_id=0, has_side_effects=True
        ),
    )(slots, labels, coefficients, potential, to_values, two_scale, octant, xk, yz_kernels)


def solution(mesh):
    spread = P(("oct", "sub"), None)
    placed = (spread, spread, P(), P(), P(), P(), spread, spread, P(("oct", "sub")), P(("oct", "sub")))
    return jax.shard_map(
        shards, mesh=mesh, in_specs=placed, out_specs=(spread, spread), check_vma=False
    )
```

time: 168 us -> 132 us (0.79)
  Pallas kernels: 161 us -> 128 us
  local copies, waits for them, and re-layouts: 4.89 us -> 3.04 us
    pallas_call x1, Pallas kernels: 144 us -> 126 us  [shards(): pl.pallas_call(main_kernel, out_shape=(jax.ShapeDtypeStruct((BOXES, K * P...]
    pallas_call x1, Pallas kernels: 16.7 us -> 2.33 us  [shards(): pl.pallas_call(route_kernel, out_shape=(ints((1, TABLE)), ints((DEVICES,...]
    reshape x2 -> x0, local copies, waits for them, and re-layouts: 1.85 us -> none  [shards(): xk = x_kernels.transpose(1, 0, 2).reshape(3, K, TERMS * K)]
where the time goes in v3:
time: 132 us
  Pallas kernels  128 us (97%)
  local copies, waits for them, and re-layouts  3.04 us (2%)
    pallas_call x1, Pallas kernels, shards(): pl.pallas_call(main_kernel, out_shape=(jax.ShapeDtypeStruct((BOXES, K * P...  126 us
    unnamed x2, local copies, waits for them, and re-layouts  3.04 us

profile of v3, /device:TPU:0, one launch (start us, length us, event | category | flops | bytes accessed | tf_op | source)
XLA Modules:
  0.0 131.5 jit_solution(3910809730977861498)
XLA Ops:
  0.6 2.3 %shard_map.113 = (s32[1,768]{1,0:T(1,128)}, s32[128,1,256]{2,1,0:T(1,128)}) custom-call(s32[16,16]{1,0:T(8,128)} %dest_ref.1, s32[16,16]{1,0:T(8,128)} %disp_ref.1, s32[1,16]{1,0:T(1,128)} %bitcast.7), custom_call_target="tpu_custom_call" | custom-call | tf_op jit(solution)/shard_map/pallas_call | solution.py:477
  3.0 125.5 %shard_map.114 = (f32[16,4096]{1,0:T(8,128)}, f32[2,4096]{1,0:T(2,128)}) custom-call(s32[1,768]{1,0:T(1,128)} %get-tuple-element.4.slots_ref, s32[128,1,256]{2,1,0:T(1,128)} %get-tuple-element.5.labels_ref, f32[16,4096]{1,0:T(8,128)} %coef_ref.1, f32[16,4096]{1,0:T(8,128)} %pot_ref.1, f32[16,16]{1,0:T(8,128)} %table_ref.1, f32[2,16,16]{2,1,0:T(8,128)} %scale_ref.1, ...), custom_call_target="tpu_custom_call" | custom-call | tf_op jit(solution)/shard_map/pallas_call | solution.py:485
  128.5 1.7 %copy.14 = f32[16,4096]{1,0:T(8,128)} copy(f32[16,4096]{1,0:T(8,128)} %get-tuple-element.8) | data formatting | bytes 524288
  130.2 1.4 %copy.15 = f32[2,4096]{1,0:T(2,128)} copy(f32[2,4096]{1,0:T(2,128)} %get-tuple-element.9) | data formatting | bytes 65536

commit v4 on v3

--- a/solution.py
+++ b/solution.py
@@ -118,6 +118,12 @@
     return mm3(pairs[2], split(mm3(split(product), pairs[3]))).astype(BF16)
 
 
+def corrected(gathered, matched, octants, down_mats, sides):
+    inner = by_octant(matched[...].reshape(ROWS, PLANE), octants, down_mats)
+    g_hi, g_lo = split(gathered)
+    return mm(sides[2], g_hi) + mm(sides[2], g_lo) - mm(sides[1], inner.astype(BF16))
+
+
 def rows_of(ref):
     return jnp.concatenate([ref[:, x * PLANE : (x + 1) * PLANE] for x in range(K)], axis=0)
 
@@ -232,9 +238,9 @@
 
 def main_kernel(
     slots_ref, labels_ref, coef_ref, pot_ref, table_ref, scale_ref, octant_ref, xk_ref, yz_hbm,
-    field_ref, parents_ref,
+    gathered_ref, matched, sums_ref, down_mats, sides,
     yz_buf, partial, send, recv, up_send, up_recv, down_send, down_recv, tags,
-    mats, up_mats, down_mats, sides, lifted, matched, xk,
+    mats, up_mats, lifted, xk,
     yz_sem, tag_sem, send_sem, recv_sem, tree_sem,
 ):
     for m in range(TERMS):
@@ -410,10 +416,8 @@
             block = up_recv[it, h * UP_BATCH : (h + 1) * UP_BATCH].reshape(ROWS, PLANE)
             sums = sums + mm(member.astype(BF16), block)
         if it == ITERS - 1:
-            for p in range(2):
-                for i in range(K):
-                    at = p * K + i
-                    parents_ref[p : p + 1, i * PLANE : (i + 1) * PLANE] = sums[at : at + 1, :]
+            sums_ref[...] = sums
+            gathered_ref[...] = gathered
 
         if it > 0:
             left(down_send.at[pl.ds(1, GROUP - 1)], tree_sem.at[it - 1, 2], tree_sem.at[0, 3])
@@ -438,20 +442,26 @@
 
         for b in range(BOXES):
             matched[b] = down_recv[it, slots_ref[0, HOME + b]]
-        inner = by_octant(matched[...].reshape(ROWS, PLANE), octants, down_mats)
-        g_hi, g_lo = split(gathered)
-        current = mm(sides[2], g_hi) + mm(sides[2], g_lo) - mm(sides[1], inner.astype(BF16))
         if it < ITERS - 1:
+            current = corrected(gathered, matched, octants, down_mats, sides)
             source = source_of(current, pot_ref, mats)
-        else:
-            for x in range(K):
-                field_ref[:, x * PLANE : (x + 1) * PLANE] = current[x * BOXES : (x + 1) * BOXES, :]
 
     last = ITERS - 1
     left(tags.at[pl.ds(1, DEVICES - 1)], tag_sem.at[0], tag_sem.at[1])
     left(send.at[:, pl.ds(1, DEVICES - 1)], send_sem.at[last], recv_sem.at[0, 0, 0])
     left(up_send.at[pl.ds(1, GROUP - 1)], tree_sem.at[last, 0], tree_sem.at[0, 1])
     left(down_send.at[pl.ds(1, GROUP - 1)], tree_sem.at[last, 2], tree_sem.at[0, 3])
+
+
+def last_kernel(gathered_ref, matched, sums_ref, down_mats, sides, octant_ref, field_ref, parents_ref):
+    octants = octant_rows(octant_ref, "high") % 4
+    current = corrected(gathered_ref[...], matched, octants, down_mats, sides)
+    for x in range(K):
+        field_ref[:, x * PLANE : (x + 1) * PLANE] = current[x * BOXES : (x + 1) * BOXES, :]
+    for p in range(2):
+        for i in range(K):
+            at = p * K + i
+            parents_ref[p : p + 1, i * PLANE : (i + 1) * PLANE] = sums_ref[at : at + 1, :]
 
 
 SMEM = pl.BlockSpec(memory_space=pltpu.SMEM)
@@ -482,14 +492,18 @@
     )(dest_box, disp_ids, parent_of.reshape(1, BOXES))
     mat = (ROWS, ROWS)
     dma = pltpu.SemaphoreType.DMA
-    return pl.pallas_call(
+    shape = jax.ShapeDtypeStruct
+    parts = pl.pallas_call(
         main_kernel,
         out_shape=(
-            jax.ShapeDtypeStruct((BOXES, K * PLANE), F32),
-            jax.ShapeDtypeStruct((2, K * PLANE), F32),
+            shape(mat, F32),
+            shape((BOXES, K, PLANE), BF16),
+            shape((2 * K, PLANE), F32),
+            shape((4, *mat), BF16),
+            shape((3, *mat), BF16),
         ),
         in_specs=[SMEM] + [VMEM] * 7 + [ANY],
-        out_specs=(VMEM, VMEM),
+        out_specs=(VMEM,) * 5,
         scratch_shapes=[
             pltpu.VMEM((TERMS, PLANE, WIDE), BF16),
             pltpu.VMEM((SHIFTS * BOXES, TERMS * K, PLANE), BF16),
@@ -502,9 +516,6 @@
             pltpu.VMEM((DEVICES, 1, PLANE), I32),
             pltpu.VMEM((8, *mat), BF16),
             pltpu.VMEM((4, *mat), BF16),
-            pltpu.VMEM((4, *mat), BF16),
-            pltpu.VMEM((3, *mat), BF16),
-            pltpu.VMEM((BOXES, K, PLANE), BF16),
             pltpu.VMEM((BOXES, K, PLANE), BF16),
             pltpu.VMEM((3, K, TERMS * K), BF16),
             dma((TERMS,)),
@@ -517,6 +528,12 @@
             vmem_limit_bytes=VMEM_LIMIT, collective_id=0, has_side_effects=True
         ),
     )(slots, labels, coefficients, potential, to_values, two_scale, octant, xk, yz_kernels)
+    return pl.pallas_call(
+        last_kernel,
+        out_shape=(shape((BOXES, K * PLANE), F32), shape((2, K * PLANE), F32)),
+        in_specs=[VMEM] * 6,
+        out_specs=(VMEM, VMEM),
+    )(*parts, octant)
 
 
 def solution(mesh):

time: 132 us -> 131 us (level)
  local copies, waits for them, and re-layouts: 3.04 us -> 0 us
  Pallas kernels: 128 us -> 130 us
    unnamed x2 -> x0, local copies, waits for them, and re-layouts: 3.04 us -> none
    pallas_call x1 -> x2, Pallas kernels: 126 us -> 128 us  [the longest x1 125 us: shards(): pl.pallas_call(main_kernel, out_shape=(shape(mat, F32), shape((BOXES, K,...]
where the time goes in v4:
time: 131 us
  Pallas kernels  130 us (99%)
    pallas_call x1, Pallas kernels, shards(): pl.pallas_call(main_kernel, out_shape=(shape(mat, F32), shape((BOXES, K,...  125 us

profile of v4, /device:TPU:0, one launch (start us, length us, event | category | flops | bytes accessed | tf_op | source)
XLA Modules:
  0.0 130.9 jit_solution(6871000056053643508)
XLA Ops:
  0.6 2.3 %shard_map.113 = (s32[1,768]{1,0:T(1,128)}, s32[128,1,256]{2,1,0:T(1,128)}) custom-call(s32[16,16]{1,0:T(8,128)} %dest_ref.1, s32[16,16]{1,0:T(8,128)} %disp_ref.1, s32[1,16]{1,0:T(1,128)} %bitcast.8), custom_call_target="tpu_custom_call" | custom-call | tf_op jit(solution)/shard_map/pallas_call | solution.py:487
  3.0 125.3 %shard_map.114 = (f32[256,256]{1,0:T(8,128)}, bf16[16,16,256]{2,1,0:T(8,128)(2,1)}, f32[32,256]{1,0:T(8,128)}, bf16[4,256,256]{2,1,0:T(8,128)(2,1)}, bf16[3,256,256]{2,1,0:T(8,128)(2,1)}) custom-call(s32[1,768]{1,0:T(1,128)} %get-tuple-element.9.slots_ref, s32[128,1,256]{2,1,0:T(1,128)} %get-tuple-element.10.labels_ref, f32[16,4096]{1,0:T(8,128)} %coef_ref.1, ...), custom_call_target="tpu_custom_call" | custom-call | tf_op jit(solution)/shard_map/pallas_call | solution.py:496
  128.3 2.6 %shard_map.115 = (f32[16,4096]{1,0:T(8,128)}, f32[2,4096]{1,0:T(2,128)}) custom-call(f32[256,256]{1,0:T(8,128)} %get-tuple-element.11.gathered_ref, bf16[16,16,256]{2,1,0:T(8,128)(2,1)} %get-tuple-element.12.matched, f32[32,256]{1,0:T(8,128)} %get-tuple-element.13.sums_ref, bf16[4,256,256]{2,1,0:T(8,128)(2,1)} %get-tuple-element.14.down_mats, ...), custom_call_target="tpu_custom_call" | custom-call | tf_op jit(solution)/shard_map/pallas_call | solution.py:531

commit v5 on v4

--- a/solution.py
+++ b/solution.py
@@ -112,10 +112,10 @@
 
 
 def source_of(current, pot_ref, mats):
-    pairs = [(mats[2 * n], mats[2 * n + 1]) for n in range(4)]
+    pairs = [(mats[2 * n], mats[2 * n + 1]) for n in range(2)]
     values = mm3(pairs[0], split(mm3(split(current), pairs[1])))
     product = values * (rows_of(pot_ref) + 0.25 * values * values)
-    return mm3(pairs[2], split(mm3(split(product), pairs[3]))).astype(BF16)
+    return mm(mats[2 * 2], mm(product.astype(BF16), mats[2 * 3]).astype(BF16)).astype(BF16)
 
 
 def corrected(gathered, matched, octants, down_mats, sides):

time: 131 us -> 131 us (level)
  no operation moved by 1% of the time
where the time goes in v5:
time: 131 us
  Pallas kernels  130 us (99%)
    pallas_call x1, Pallas kernels, shards(): pl.pallas_call(main_kernel, out_shape=(shape(mat, F32), shape((BOXES, K,...  125 us

profile of v5, /device:TPU:0, one launch (start us, length us, event | category | flops | bytes accessed | tf_op | source)
XLA Modules:
  0.0 130.8 jit_solution(13436247455346654868)
XLA Ops:
  0.6 2.3 %shard_map.113 = (s32[1,768]{1,0:T(1,128)}, s32[128,1,256]{2,1,0:T(1,128)}) custom-call(s32[16,16]{1,0:T(8,128)} %dest_ref.1, s32[16,16]{1,0:T(8,128)} %disp_ref.1, s32[1,16]{1,0:T(1,128)} %bitcast.8), custom_call_target="tpu_custom_call" | custom-call | tf_op jit(solution)/shard_map/pallas_call | solution.py:487
  3.0 125.3 %shard_map.114 = (f32[256,256]{1,0:T(8,128)}, bf16[16,16,256]{2,1,0:T(8,128)(2,1)}, f32[32,256]{1,0:T(8,128)}, bf16[4,256,256]{2,1,0:T(8,128)(2,1)}, bf16[3,256,256]{2,1,0:T(8,128)(2,1)}) custom-call(s32[1,768]{1,0:T(1,128)} %get-tuple-element.9.slots_ref, s32[128,1,256]{2,1,0:T(1,128)} %get-tuple-element.10.labels_ref, f32[16,4096]{1,0:T(8,128)} %coef_ref.1, ...), custom_call_target="tpu_custom_call" | custom-call | tf_op jit(solution)/shard_map/pallas_call | solution.py:496
  128.2 2.6 %shard_map.115 = (f32[16,4096]{1,0:T(8,128)}, f32[2,4096]{1,0:T(2,128)}) custom-call(f32[256,256]{1,0:T(8,128)} %get-tuple-element.11.gathered_ref, bf16[16,16,256]{2,1,0:T(8,128)(2,1)} %get-tuple-element.12.matched, f32[32,256]{1,0:T(8,128)} %get-tuple-element.13.sums_ref, bf16[4,256,256]{2,1,0:T(8,128)(2,1)} %get-tuple-element.14.down_mats, ...), custom_call_target="tpu_custom_call" | custom-call | tf_op jit(solution)/shard_map/pallas_call | solution.py:531

commit v6 on v4

--- a/solution.py
+++ b/solution.py
@@ -332,7 +332,7 @@
                 lax.fori_loop(0, BURSTS // 3, telling, 0)
                 lax.fori_loop(BURSTS // 3, TERMS // 2, step, 0)
             else:
-                lax.fori_loop(0, TERMS // 2, step, 0)
+                lax.fori_loop(0, TERMS // 2, step, 0, unroll=2)
 
             def ship(n, skip, it=it, h=h):
                 devices = burst_of(jnp.int32(n), 1)

time: 131 us -> 130 us (level)
    pallas_call x1, Pallas kernels: 125 us -> 124 us  [shards(): pl.pallas_call(main_kernel, out_shape=(shape(mat, F32), shape((BOXES, K,...]
where the time goes in v6:
time: 130 us; the launch traced here: 129 us
  Pallas kernels  129 us (99%)
    pallas_call x1, Pallas kernels, shards(): pl.pallas_call(main_kernel, out_shape=(shape(mat, F32), shape((BOXES, K,...  124 us

profile of v6, /device:TPU:0, one launch (start us, length us, event | category | flops | bytes accessed | tf_op | source)
XLA Modules:
  0.0 129.5 jit_solution(18246341513162640175)
XLA Ops:
  0.6 2.3 %shard_map.113 = (s32[1,768]{1,0:T(1,128)}, s32[128,1,256]{2,1,0:T(1,128)}) custom-call(s32[16,16]{1,0:T(8,128)} %dest_ref.1, s32[16,16]{1,0:T(8,128)} %disp_ref.1, s32[1,16]{1,0:T(1,128)} %bitcast.8), custom_call_target="tpu_custom_call" | custom-call | tf_op jit(solution)/shard_map/pallas_call | solution.py:487
  3.0 123.9 %shard_map.114 = (f32[256,256]{1,0:T(8,128)}, bf16[16,16,256]{2,1,0:T(8,128)(2,1)}, f32[32,256]{1,0:T(8,128)}, bf16[4,256,256]{2,1,0:T(8,128)(2,1)}, bf16[3,256,256]{2,1,0:T(8,128)(2,1)}) custom-call(s32[1,768]{1,0:T(1,128)} %get-tuple-element.9.slots_ref, s32[128,1,256]{2,1,0:T(1,128)} %get-tuple-element.10.labels_ref, f32[16,4096]{1,0:T(8,128)} %coef_ref.1, ...), custom_call_target="tpu_custom_call" | custom-call | tf_op jit(solution)/shard_map/pallas_call | solution.py:496
  126.9 2.6 %shard_map.115 = (f32[16,4096]{1,0:T(8,128)}, f32[2,4096]{1,0:T(2,128)}) custom-call(f32[256,256]{1,0:T(8,128)} %get-tuple-element.11.gathered_ref, bf16[16,16,256]{2,1,0:T(8,128)(2,1)} %get-tuple-element.12.matched, f32[32,256]{1,0:T(8,128)} %get-tuple-element.13.sums_ref, bf16[4,256,256]{2,1,0:T(8,128)(2,1)} %get-tuple-element.14.down_mats, ...), custom_call_target="tpu_custom_call" | custom-call | tf_op jit(solution)/shard_map/pallas_call | solution.py:531
